TPU v7x, 256 devices: a whole 4x4x8 slice. The times are simulated.
256 devices in a mesh: img: 16 (over y_lo, z), gx: 4 (over y_hi, core), gy: 4 (over x).
Axes of the slice: x: 4, y: 4 (y_hi: 2, y_lo: 2; y = y_hi * 2 + y_lo), z: 8, core: 2. Of those that a mesh axis runs over, the one named last changes fastest.
Arguments:
- magnetization: float32 [16, 3, 16, 64, 512], P('img', None, None, 'gy', 'gx'), may hold values from -1 to 1, as said below
- lower_image: int32 [16], replicated, may hold values from 0 to 14, as said below
- image_weights: float32 [15], replicated, may hold values from 0.5 to 2
- regions: int32 [16, 64, 512], P(None, 'gy', 'gx'), may hold values from 0 to 7
- anisotropy: float32 [8], replicated, may hold values from 0.5 to 4
- damping: float32 [8], replicated, may hold values from 0.05 to 0.5
Outputs:
- evolved: float32 [16, 3, 16, 64, 512], P('img', None, None, 'gy', 'gx')
Inputs may be any that keep to these rules, and one draw needn't show every extreme that they name: `lower_image`: lower_image_j is j - 1 or j; it is 0 for image 0 and 14 for the last image. `magnetization`: every cell holds a unit vector, and in every cell neighbouring images make an angle under 90 degrees.
All inputs are finite; a program needn't handle non-finite values.
Results may differ from a plain program's by a relative error of at most 0.000024.
Values sent between devices are 32-bit elements; how exact they have to be, the bound alone decides.
A program may use at most 64 MiB of HBM per device.

v0:
```python
import jax
import jax.numpy as jnp
from jax import lax
from jax.sharding import PartitionSpec as P

STEPS = 4


eps = 1e-06
time_step = 0.05


def padded_2(cells, sides, width, closed):
    for axis, dim in sides:
        count = lax.axis_size(axis)
        ends = count if closed else count - 1
        head = lax.slice_in_dim(cells, 0, width, axis=dim)
        tail = lax.slice_in_dim(cells, cells.shape[dim] - width, cells.shape[dim], axis=dim)
        cells = jnp.concatenate(
            [
                lax.ppermute(tail, axis, [(i, (i + 1) % count) for i in range(ends)]),
                cells,
                lax.ppermute(head, axis, [((i + 1) % count, i) for i in range(ends)]),
            ],
            axis=dim,
        )
    return cells


def normalize(field):
    return (
        field
        * lax.rsqrt(
            field[..., 0, :, :, :] ** 2 + field[..., 1, :, :, :] ** 2 + field[..., 2, :, :, :] ** 2
        )[..., None, :, :, :]
    )


def laplacian(padded):
    center = padded[..., 1:-1, 1:-1]
    plane = (
        padded[..., 1:-1, 2:]
        + padded[..., 1:-1, :-2]
        + padded[..., 2:, 1:-1]
        + padded[..., :-2, 1:-1]
        - 4.0 * center
    )
    upper = jnp.concatenate([center[..., 1:, :, :], center[..., -1:, :, :]], axis=-3)
    lower = jnp.concatenate([center[..., :1, :, :], center[..., :-1, :, :]], axis=-3)
    return plane + (upper + lower - 2.0 * center)


def torque_rate(field, lap, aniso, damp):
    mx, my, mz = (field[..., 0, :, :, :], field[..., 1, :, :, :], field[..., 2, :, :, :])
    hx, hy = (lap[..., 0, :, :, :], lap[..., 1, :, :, :])
    hz = lap[..., 2, :, :, :] + 2.0 * aniso * mz
    cx = my * hz - mz * hy
    cy = mz * hx - mx * hz
    cz = mx * hy - my * hx
    dx = my * cz - mz * cy
    dy = mz * cx - mx * cz
    dz = mx * cy - my * cx
    scale = -1.0 / (1.0 + damp * damp)
    return jnp.stack(
        [scale * (cx + damp * dx), scale * (cy + damp * dy), scale * (cz + damp * dz)], axis=-4
    )


def lookup(regions, anisotropy, damping):
    aniso = jnp.zeros(regions.shape, jnp.float32)
    damp = jnp.zeros(regions.shape, jnp.float32)
    for region in range(anisotropy.shape[0]):
        inside = regions == region
        aniso = jnp.where(inside, anisotropy[region], aniso)
        damp = jnp.where(inside, damping[region], damp)
    return (aniso, damp)


def face_halo(field):
    return padded_2(field, (("gx", 4), ("gy", 3)), 1, True)


def body(magnetization, lower_image, image_weights, regions, anisotropy, damping):
    local = magnetization.shape[0]
    images_all = local * lax.axis_size("img")
    first_image = lax.axis_index("img") * local
    extended = padded_2(magnetization, (("img", 0),), 1, False)
    partial_value = jnp.sum((extended[1:-1] - extended[:-2]) ** 2, axis=(1, 2, 3, 4))
    summed = lax.psum(partial_value, ("gx", "gy"))
    squares = lax.all_gather(summed, "img", axis=0, tiled=True)
    position = jnp.arange(images_all)
    lengths = jnp.where(position >= 1, jnp.sqrt(squares + eps), jnp.float32(0.0))
    arc = jnp.cumsum(lengths)
    total = arc[-1]
    shares = jnp.concatenate([jnp.zeros((1,), jnp.float32), jnp.cumsum(image_weights)])
    target = shares / shares[-1]
    index = first_image + 0
    lower = lax.dynamic_index_in_dim(lower_image, index, 0, False)
    here_arc = lax.dynamic_index_in_dim(arc, lower, 0, False)
    gap = lax.dynamic_index_in_dim(lengths, lower + 1, 0, False)
    aim = lax.dynamic_index_in_dim(target, index, 0, False)
    weight = jnp.clip((aim * total - here_arc) / gap, -0.5, 1.5)
    offset = lower - first_image + 1
    below = lax.dynamic_index_in_dim(extended, offset, 0, False)
    above = lax.dynamic_index_in_dim(extended, offset + 1, 0, False)
    new_images = [normalize((1.0 - weight) * below + weight * above)]
    field = jnp.stack(new_images)
    aniso, damp = lookup(regions, anisotropy, damping)
    for step in range(STEPS):
        first_rate = torque_rate(field, laplacian(face_halo(field)), aniso, damp)
        predicted = field + time_step * first_rate
        second_rate = torque_rate(predicted, laplacian(face_halo(predicted)), aniso, damp)
        field = normalize(field + 0.5 * time_step * (first_rate + second_rate))
    return field


def solution(mesh):
    placed = (P("img", None, None, "gy", "gx"), P(), P(), P(None, "gy", "gx"), P(), P())
    return jax.shard_map(
        body,
        mesh=mesh,
        in_specs=placed,
        out_specs=P("img", None, None, "gy", "gx"),
        check_vma=False,
    )
```

profile of v0, /device:TPU:8, one launch (start us, length us, event | category | flops | bytes accessed | tf_op | source)
XLA Modules:
  0.0 283.4 jit_solution(3402406977408648769)
XLA Ops:
  0.0 3.9 %collective-permute-start = (f32[1,3,16,16,128]{4,3,2,1,0:T(8,128)}, f32[1,3,16,16,128]{4,3,2,1,0:T(8,128)S(1)}, u32[]{:S(2)}, u32[]{:S(2)}) collective-permute-start(f32[1,3,16,16,128]{4,3,2,1,0:T(8,128)} %param.6), channel_id=1, source_target_pairs={{0,16},{16,32},{32,48},{48,64},{64,80},{80,96},{96,112},{112,128},... | collective-permute-start | bytes 1179656 | tf_op jit(solution)/shard_map/ppermute | solution.py:21
  4.0 5.7 %collective-permute-start.1 = (f32[1,3,16,16,128]{4,3,2,1,0:T(8,128)}, f32[1,3,16,16,128]{4,3,2,1,0:T(8,128)S(1)}, u32[]{:S(2)}, u32[]{:S(2)}) collective-permute-start(f32[1,3,16,16,128]{4,3,2,1,0:T(8,128)} %param.6), channel_id=1, source_target_pairs={{16,0},{32,16},{48,32},{64,48},{80,64},{96,80},{112,96},{128,112},... | collective-permute-start | bytes 1179656 | tf_op jit(solution)/shard_map/ppermute | solution.py:23
  25.0 37.7 %psum.7 = f32[1]{0:T(128)} all-reduce(f32[1]{0:T(128)} %bitcast.4), channel_id=1, replica_groups=mesh['img'=16,'gx'=4,'gy'=4] {'gx','gy'}, use_global_device_ids=true, to_apply=%region_2.3 | all-reduce | flops 1 | bytes 8 | tf_op jit(solution)/shard_map/psum | solution.py:89
  64.0 32.9 %all-reduce = f32[16]{0:T(128)S(1)} all-reduce(f32[16]{0:T(128)S(1)} %dynamic-update-slice), channel_id=1, replica_groups=mesh['img'=16,'gx'=4,'gy'=4] {'img'}, use_global_device_ids=true, to_apply=%add | all-reduce | flops 16 | bytes 128
  101.4 3.2 %collective-permute-start.2 = (f32[1,3,16,16,1]{4,3,2,1,0:T(8,128)S(1)}, f32[1,3,16,16,1]{4,3,2,1,0:T(8,128)S(1)}, u32[]{:S(2)}, u32[]{:S(2)}) collective-permute-start(f32[1,3,16,16,1]{4,3,2,1,0:T(8,128)S(1)} %get-tuple-element.118), channel_id=1, source_target_pairs={{4,0},{8,4},{12,8},{0,12},{5,1},{9,5},{13,9},{1,13},{6,2},{10,6},{... | collective-permute-start | bytes 9224 | tf_op jit(solution)/shard_map/ppermute | solution.py:23
  104.7 9.5 %collective-permute-done.3 = f32[1,3,16,16,1]{4,3,2,1,0:T(8,128)S(1)} collective-permute-done((f32[1,3,16,16,1]{4,3,2,1,0:T(8,128)S(1)}, f32[1,3,16,16,1]{4,3,2,1,0:T(8,128)S(1)}, u32[]{:S(2)}, u32[]{:S(2)}) %collective-permute-start.3) | collective-permute-done | bytes 3104 | tf_op jit(solution)/shard_map/ppermute | solution.py:21
  120.8 10.2 %multiply_bitcast_fusion.23 = (f32[1,1,16,16,128]{4,3,2,1,0:T(8,128)S(1)}, f32[16,16,128]{2,1,0:T(8,128)S(1)}, f32[16,16,128]{2,1,0:T(8,128)S(1)}, f32[16,16,128...) fusion(f32[1,3,16,16,128]{4,3,2,1,0:T(8,128)S(1)} %broadcast_multiply_fusion.4, ...), kind=kLoop, calls=%fused_computation.282 | loop fusion | flops 1212416 | bytes 1835072 | tf_op jit(solution)/shard_map/stack | solution.py:64
  131.5 3.2 %collective-permute-start.6 = (f32[1,3,16,16,1]{4,3,2,1,0:T(8,128)S(1)}, f32[1,3,16,16,1]{4,3,2,1,0:T(8,128)S(1)}, u32[]{:S(2)}, u32[]{:S(2)}) collective-permute-start(f32[1,3,16,16,1]{4,3,2,1,0:T(8,128)S(1)} %get-tuple-element.112), channel_id=1, source_target_pairs={{4,0},{8,4},{12,8},{0,12},{5,1},{9,5},{13,9},{1,13},{6,2},{10,6},{... | collective-permute-start | bytes 9224 | tf_op jit(solution)/shard_map/ppermute | solution.py:23
  134.8 9.6 %collective-permute-done.7 = f32[1,3,16,16,1]{4,3,2,1,0:T(8,128)S(1)} collective-permute-done((f32[1,3,16,16,1]{4,3,2,1,0:T(8,128)S(1)}, f32[1,3,16,16,1]{4,3,2,1,0:T(8,128)S(1)}, u32[]{:S(2)}, u32[]{:S(2)}) %collective-permute-start.7) | collective-permute-done | bytes 3104 | tf_op jit(solution)/shard_map/ppermute | solution.py:21
  146.9 2.1 collective-permute-done.8
  151.8 3.5 %collective-permute-start.10 = (f32[1,3,16,16,1]{4,3,2,1,0:T(8,128)S(1)}, f32[1,3,16,16,1]{4,3,2,1,0:T(8,128)S(1)}, u32[]{:S(2)}, u32[]{:S(2)}) collective-permute-start(f32[1,3,16,16,1]{4,3,2,1,0:T(8,128)S(1)} %get-tuple-element.106), channel_id=1, source_target_pairs={{4,0},{8,4},{12,8},{0,12},{5,1},{9,5},{13,9},{1,13},{6,2},{10,6},{... | collective-permute-start | bytes 9224 | tf_op jit(solution)/shard_map/ppermute | solution.py:23
  155.3 9.3 %collective-permute-done.11 = f32[1,3,16,16,1]{4,3,2,1,0:T(8,128)S(1)} collective-permute-done((f32[1,3,16,16,1]{4,3,2,1,0:T(8,128)S(1)}, f32[1,3,16,16,1]{4,3,2,1,0:T(8,128)S(1)}, u32[]{:S(2)}, u32[]{:S(2)}) %collective-permute-start.11) | collective-permute-done | bytes 3104 | tf_op jit(solution)/shard_map/ppermute | solution.py:21
  171.9 3.2 %collective-permute-start.14 = (f32[1,3,16,16,1]{4,3,2,1,0:T(8,128)S(1)}, f32[1,3,16,16,1]{4,3,2,1,0:T(8,128)S(1)}, u32[]{:S(2)}, u32[]{:S(2)}) collective-permute-start(f32[1,3,16,16,1]{4,3,2,1,0:T(8,128)S(1)} %get-tuple-element.100), channel_id=1, source_target_pairs={{4,0},{8,4},{12,8},{0,12},{5,1},{9,5},{13,9},{1,13},{6,2},{10,6},{... | collective-permute-start | bytes 9224 | tf_op jit(solution)/shard_map/ppermute | solution.py:23
  175.2 9.5 %collective-permute-done.15 = f32[1,3,16,16,1]{4,3,2,1,0:T(8,128)S(1)} collective-permute-done((f32[1,3,16,16,1]{4,3,2,1,0:T(8,128)S(1)}, f32[1,3,16,16,1]{4,3,2,1,0:T(8,128)S(1)}, u32[]{:S(2)}, u32[]{:S(2)}) %collective-permute-start.15) | collective-permute-done | bytes 3104 | tf_op jit(solution)/shard_map/ppermute | solution.py:21
  192.9 3.2 %collective-permute-start.18 = (f32[1,3,16,16,1]{4,3,2,1,0:T(8,128)S(1)}, f32[1,3,16,16,1]{4,3,2,1,0:T(8,128)S(1)}, u32[]{:S(2)}, u32[]{:S(2)}) collective-permute-start(f32[1,3,16,16,1]{4,3,2,1,0:T(8,128)S(1)} %get-tuple-element.94), channel_id=1, source_target_pairs={{4,0},{8,4},{12,8},{0,12},{5,1},{9,5},{13,9},{1,13},{6,2},{10,6},{... | collective-permute-start | bytes 9224 | tf_op jit(solution)/shard_map/ppermute | solution.py:23
  196.2 9.3 %collective-permute-done.19 = f32[1,3,16,16,1]{4,3,2,1,0:T(8,128)S(1)} collective-permute-done((f32[1,3,16,16,1]{4,3,2,1,0:T(8,128)S(1)}, f32[1,3,16,16,1]{4,3,2,1,0:T(8,128)S(1)}, u32[]{:S(2)}, u32[]{:S(2)}) %collective-permute-start.19) | collective-permute-done | bytes 3104 | tf_op jit(solution)/shard_map/ppermute | solution.py:21
  206.1 10.6 %collective-permute-start.21 = (f32[1,3,16,1,130]{4,3,2,1,0:T(1,128)S(1)}, f32[1,3,16,1,130]{4,3,2,1,0:T(1,128)S(1)}, u32[]{:S(2)}, u32[]{:S(2)}) collective-permute-start(f32[1,3,16,1,130]{4,3,2,1,0:T(1,128)S(1)} %get-tuple-element.46), channel_id=1, source_target_pairs={{0,1},{1,2},{2,3},{3,0},{4,5},{5,6},{6,7},{7,4},{8,9},{9,10},{10,1... | collective-permute-start | bytes 74888 | tf_op jit(solution)/shard_map/ppermute | solution.py:21
  216.7 3.6 %collective-permute-done.21 = f32[1,3,16,1,130]{4,3,2,1,0:T(1,128)S(1)} collective-permute-done((f32[1,3,16,1,130]{4,3,2,1,0:T(1,128)S(1)}, f32[1,3,16,1,130]{4,3,2,1,0:T(1,128)S(1)}, u32[]{:S(2)}, u32[]{:S(2)}) %collective-permute-start.21) | collective-permute-done | bytes 24992 | tf_op jit(solution)/shard_map/ppermute | solution.py:21
  221.8 3.2 %collective-permute-start.22 = (f32[1,3,16,16,1]{4,3,2,1,0:T(8,128)S(1)}, f32[1,3,16,16,1]{4,3,2,1,0:T(8,128)S(1)}, u32[]{:S(2)}, u32[]{:S(2)}) collective-permute-start(f32[1,3,16,16,1]{4,3,2,1,0:T(8,128)S(1)} %get-tuple-element.88), channel_id=1, source_target_pairs={{4,0},{8,4},{12,8},{0,12},{5,1},{9,5},{13,9},{1,13},{6,2},{10,6},{... | collective-permute-start | bytes 9224 | tf_op jit(solution)/shard_map/ppermute | solution.py:23
  225.1 9.2 %collective-permute-done.23 = f32[1,3,16,16,1]{4,3,2,1,0:T(8,128)S(1)} collective-permute-done((f32[1,3,16,16,1]{4,3,2,1,0:T(8,128)S(1)}, f32[1,3,16,16,1]{4,3,2,1,0:T(8,128)S(1)}, u32[]{:S(2)}, u32[]{:S(2)}) %collective-permute-start.23) | collective-permute-done | bytes 3104 | tf_op jit(solution)/shard_map/ppermute | solution.py:21
  242.0 3.2 %collective-permute-start.26 = (f32[1,3,16,16,1]{4,3,2,1,0:T(8,128)S(1)}, f32[1,3,16,16,1]{4,3,2,1,0:T(8,128)S(1)}, u32[]{:S(2)}, u32[]{:S(2)}) collective-permute-start(f32[1,3,16,16,1]{4,3,2,1,0:T(8,128)S(1)} %get-tuple-element.82), channel_id=1, source_target_pairs={{4,0},{8,4},{12,8},{0,12},{5,1},{9,5},{13,9},{1,13},{6,2},{10,6},{... | collective-permute-start | bytes 9224 | tf_op jit(solution)/shard_map/ppermute | solution.py:23
  245.3 9.3 %collective-permute-done.27 = f32[1,3,16,16,1]{4,3,2,1,0:T(8,128)S(1)} collective-permute-done((f32[1,3,16,16,1]{4,3,2,1,0:T(8,128)S(1)}, f32[1,3,16,16,1]{4,3,2,1,0:T(8,128)S(1)}, u32[]{:S(2)}, u32[]{:S(2)}) %collective-permute-start.27) | collective-permute-done | bytes 3104 | tf_op jit(solution)/shard_map/ppermute | solution.py:21
  262.0 3.4 %collective-permute-start.30 = (f32[1,3,16,16,1]{4,3,2,1,0:T(8,128)S(1)}, f32[1,3,16,16,1]{4,3,2,1,0:T(8,128)S(1)}, u32[]{:S(2)}, u32[]{:S(2)}) collective-permute-start(f32[1,3,16,16,1]{4,3,2,1,0:T(8,128)S(1)} %get-tuple-element.76), channel_id=1, source_target_pairs={{4,0},{8,4},{12,8},{0,12},{5,1},{9,5},{13,9},{1,13},{6,2},{10,6},{... | collective-permute-start | bytes 9224 | tf_op jit(solution)/shard_map/ppermute | solution.py:23
  265.5 9.2 %collective-permute-done.31 = f32[1,3,16,16,1]{4,3,2,1,0:T(8,128)S(1)} collective-permute-done((f32[1,3,16,16,1]{4,3,2,1,0:T(8,128)S(1)}, f32[1,3,16,16,1]{4,3,2,1,0:T(8,128)S(1)}, u32[]{:S(2)}, u32[]{:S(2)}) %collective-permute-start.31) | collective-permute-done | bytes 3104 | tf_op jit(solution)/shard_map/ppermute | solution.py:21
  (143 shorter events, 68.1 us)
Async XLA Ops:
  0.0 23.2 %collective-permute-start = (f32[1,3,16,16,128]{4,3,2,1,0:T(8,128)}, f32[1,3,16,16,128]{4,3,2,1,0:T(8,128)S(1)}, u32[]{:S(2)}, u32[]{:S(2)}) collective-permute-start(f32[1,3,16,16,128]{4,3,2,1,0:T(8,128)} %param.6), channel_id=1, source_target_pairs={{0,16},{16,32},{32,48},{48,64},{64,80},{80,96},{96,112},{112,128},... | collective-permute-start | bytes 1179656 | tf_op jit(solution)/shard_map/ppermute | solution.py:21
  4.0 97.0 %collective-permute-start.1 = (f32[1,3,16,16,128]{4,3,2,1,0:T(8,128)}, f32[1,3,16,16,128]{4,3,2,1,0:T(8,128)S(1)}, u32[]{:S(2)}, u32[]{:S(2)}) collective-permute-start(f32[1,3,16,16,128]{4,3,2,1,0:T(8,128)} %param.6), channel_id=1, source_target_pairs={{16,0},{32,16},{48,32},{64,48},{80,64},{96,80},{112,96},{128,112},... | collective-permute-start | bytes 1179656 | tf_op jit(solution)/shard_map/ppermute | solution.py:23
  101.4 12.9 %collective-permute-start.3 = (f32[1,3,16,16,1]{4,3,2,1,0:T(8,128)S(1)}, f32[1,3,16,16,1]{4,3,2,1,0:T(8,128)S(1)}, u32[]{:S(2)}, u32[]{:S(2)}) collective-permute-start(f32[1,3,16,16,1]{4,3,2,1,0:T(8,128)S(1)} %get-tuple-element.117), channel_id=1, source_target_pairs={{0,4},{4,8},{8,12},{12,0},{1,5},{5,9},{9,13},{13,1},{2,6},{6,10},{... | collective-permute-start | bytes 9224 | tf_op jit(solution)/shard_map/ppermute | solution.py:21
  101.4 12.8 %collective-permute-start.2 = (f32[1,3,16,16,1]{4,3,2,1,0:T(8,128)S(1)}, f32[1,3,16,16,1]{4,3,2,1,0:T(8,128)S(1)}, u32[]{:S(2)}, u32[]{:S(2)}) collective-permute-start(f32[1,3,16,16,1]{4,3,2,1,0:T(8,128)S(1)} %get-tuple-element.118), channel_id=1, source_target_pairs={{4,0},{8,4},{12,8},{0,12},{5,1},{9,5},{13,9},{1,13},{6,2},{10,6},{... | collective-permute-start | bytes 9224 | tf_op jit(solution)/shard_map/ppermute | solution.py:23
  114.7 5.4 %collective-permute-start.5 = (f32[1,3,16,1,130]{4,3,2,1,0:T(1,128)S(1)}, f32[1,3,16,1,130]{4,3,2,1,0:T(1,128)S(1)}, u32[]{:S(2)}, u32[]{:S(2)}) collective-permute-start(f32[1,3,16,1,130]{4,3,2,1,0:T(1,128)S(1)} %get-tuple-element.54), channel_id=1, source_target_pairs={{0,1},{1,2},{2,3},{3,0},{4,5},{5,6},{6,7},{7,4},{8,9},{9,10},{10,1... | collective-permute-start | bytes 74888 | tf_op jit(solution)/shard_map/ppermute | solution.py:21
  131.4 13.0 %collective-permute-start.7 = (f32[1,3,16,16,1]{4,3,2,1,0:T(8,128)S(1)}, f32[1,3,16,16,1]{4,3,2,1,0:T(8,128)S(1)}, u32[]{:S(2)}, u32[]{:S(2)}) collective-permute-start(f32[1,3,16,16,1]{4,3,2,1,0:T(8,128)S(1)} %get-tuple-element.111), channel_id=1, source_target_pairs={{0,4},{4,8},{8,12},{12,0},{1,5},{5,9},{9,13},{13,1},{2,6},{6,10},{... | collective-permute-start | bytes 9224 | tf_op jit(solution)/shard_map/ppermute | solution.py:21
  131.5 12.9 %collective-permute-start.6 = (f32[1,3,16,16,1]{4,3,2,1,0:T(8,128)S(1)}, f32[1,3,16,16,1]{4,3,2,1,0:T(8,128)S(1)}, u32[]{:S(2)}, u32[]{:S(2)}) collective-permute-start(f32[1,3,16,16,1]{4,3,2,1,0:T(8,128)S(1)} %get-tuple-element.112), channel_id=1, source_target_pairs={{4,0},{8,4},{12,8},{0,12},{5,1},{9,5},{13,9},{1,13},{6,2},{10,6},{... | collective-permute-start | bytes 9224 | tf_op jit(solution)/shard_map/ppermute | solution.py:23
  144.8 5.4 %collective-permute-start.9 = (f32[1,3,16,1,130]{4,3,2,1,0:T(1,128)S(1)}, f32[1,3,16,1,130]{4,3,2,1,0:T(1,128)S(1)}, u32[]{:S(2)}, u32[]{:S(2)}) collective-permute-start(f32[1,3,16,1,130]{4,3,2,1,0:T(1,128)S(1)} %get-tuple-element.52), channel_id=1, source_target_pairs={{0,1},{1,2},{2,3},{3,0},{4,5},{5,6},{6,7},{7,4},{8,9},{9,10},{10,1... | collective-permute-start | bytes 74888 | tf_op jit(solution)/shard_map/ppermute | solution.py:21
  151.7 12.9 %collective-permute-start.11 = (f32[1,3,16,16,1]{4,3,2,1,0:T(8,128)S(1)}, f32[1,3,16,16,1]{4,3,2,1,0:T(8,128)S(1)}, u32[]{:S(2)}, u32[]{:S(2)}) collective-permute-start(f32[1,3,16,16,1]{4,3,2,1,0:T(8,128)S(1)} %get-tuple-element.105), channel_id=1, source_target_pairs={{0,4},{4,8},{8,12},{12,0},{1,5},{5,9},{9,13},{13,1},{2,6},{6,10},{... | collective-permute-start | bytes 9224 | tf_op jit(solution)/shard_map/ppermute | solution.py:21
  151.8 12.9 %collective-permute-start.10 = (f32[1,3,16,16,1]{4,3,2,1,0:T(8,128)S(1)}, f32[1,3,16,16,1]{4,3,2,1,0:T(8,128)S(1)}, u32[]{:S(2)}, u32[]{:S(2)}) collective-permute-start(f32[1,3,16,16,1]{4,3,2,1,0:T(8,128)S(1)} %get-tuple-element.106), channel_id=1, source_target_pairs={{4,0},{8,4},{12,8},{0,12},{5,1},{9,5},{13,9},{1,13},{6,2},{10,6},{... | collective-permute-start | bytes 9224 | tf_op jit(solution)/shard_map/ppermute | solution.py:23
  165.1 5.4 %collective-permute-start.13 = (f32[1,3,16,1,130]{4,3,2,1,0:T(1,128)S(1)}, f32[1,3,16,1,130]{4,3,2,1,0:T(1,128)S(1)}, u32[]{:S(2)}, u32[]{:S(2)}) collective-permute-start(f32[1,3,16,1,130]{4,3,2,1,0:T(1,128)S(1)} %get-tuple-element.50), channel_id=1, source_target_pairs={{0,1},{1,2},{2,3},{3,0},{4,5},{5,6},{6,7},{7,4},{8,9},{9,10},{10,1... | collective-permute-start | bytes 74888 | tf_op jit(solution)/shard_map/ppermute | solution.py:21
  171.8 12.9 %collective-permute-start.15 = (f32[1,3,16,16,1]{4,3,2,1,0:T(8,128)S(1)}, f32[1,3,16,16,1]{4,3,2,1,0:T(8,128)S(1)}, u32[]{:S(2)}, u32[]{:S(2)}) collective-permute-start(f32[1,3,16,16,1]{4,3,2,1,0:T(8,128)S(1)} %get-tuple-element.99), channel_id=1, source_target_pairs={{0,4},{4,8},{8,12},{12,0},{1,5},{5,9},{9,13},{13,1},{2,6},{6,10},{... | collective-permute-start | bytes 9224 | tf_op jit(solution)/shard_map/ppermute | solution.py:21
  171.9 12.8 %collective-permute-start.14 = (f32[1,3,16,16,1]{4,3,2,1,0:T(8,128)S(1)}, f32[1,3,16,16,1]{4,3,2,1,0:T(8,128)S(1)}, u32[]{:S(2)}, u32[]{:S(2)}) collective-permute-start(f32[1,3,16,16,1]{4,3,2,1,0:T(8,128)S(1)} %get-tuple-element.100), channel_id=1, source_target_pairs={{4,0},{8,4},{12,8},{0,12},{5,1},{9,5},{13,9},{1,13},{6,2},{10,6},{... | collective-permute-start | bytes 9224 | tf_op jit(solution)/shard_map/ppermute | solution.py:23
  192.8 12.7 %collective-permute-start.19 = (f32[1,3,16,16,1]{4,3,2,1,0:T(8,128)S(1)}, f32[1,3,16,16,1]{4,3,2,1,0:T(8,128)S(1)}, u32[]{:S(2)}, u32[]{:S(2)}) collective-permute-start(f32[1,3,16,16,1]{4,3,2,1,0:T(8,128)S(1)} %get-tuple-element.93), channel_id=1, source_target_pairs={{0,4},{4,8},{8,12},{12,0},{1,5},{5,9},{9,13},{13,1},{2,6},{6,10},{... | collective-permute-start | bytes 9224 | tf_op jit(solution)/shard_map/ppermute | solution.py:21
  192.9 12.6 %collective-permute-start.18 = (f32[1,3,16,16,1]{4,3,2,1,0:T(8,128)S(1)}, f32[1,3,16,16,1]{4,3,2,1,0:T(8,128)S(1)}, u32[]{:S(2)}, u32[]{:S(2)}) collective-permute-start(f32[1,3,16,16,1]{4,3,2,1,0:T(8,128)S(1)} %get-tuple-element.94), channel_id=1, source_target_pairs={{4,0},{8,4},{12,8},{0,12},{5,1},{9,5},{13,9},{1,13},{6,2},{10,6},{... | collective-permute-start | bytes 9224 | tf_op jit(solution)/shard_map/ppermute | solution.py:23
  205.9 10.8 %collective-permute-start.20 = (f32[1,3,16,1,130]{4,3,2,1,0:T(1,128)S(1)}, f32[1,3,16,1,130]{4,3,2,1,0:T(1,128)S(1)}, u32[]{:S(2)}, u32[]{:S(2)}) collective-permute-start(f32[1,3,16,1,130]{4,3,2,1,0:T(1,128)S(1)} %get-tuple-element.45), channel_id=1, source_target_pairs={{1,0},{2,1},{3,2},{0,3},{5,4},{6,5},{7,6},{4,7},{9,8},{10,9},{11,1... | collective-permute-start | bytes 74888 | tf_op jit(solution)/shard_map/ppermute | solution.py:23
  206.1 14.3 %collective-permute-start.21 = (f32[1,3,16,1,130]{4,3,2,1,0:T(1,128)S(1)}, f32[1,3,16,1,130]{4,3,2,1,0:T(1,128)S(1)}, u32[]{:S(2)}, u32[]{:S(2)}) collective-permute-start(f32[1,3,16,1,130]{4,3,2,1,0:T(1,128)S(1)} %get-tuple-element.46), channel_id=1, source_target_pairs={{0,1},{1,2},{2,3},{3,0},{4,5},{5,6},{6,7},{7,4},{8,9},{9,10},{10,1... | collective-permute-start | bytes 74888 | tf_op jit(solution)/shard_map/ppermute | solution.py:21
  221.7 12.6 %collective-permute-start.23 = (f32[1,3,16,16,1]{4,3,2,1,0:T(8,128)S(1)}, f32[1,3,16,16,1]{4,3,2,1,0:T(8,128)S(1)}, u32[]{:S(2)}, u32[]{:S(2)}) collective-permute-start(f32[1,3,16,16,1]{4,3,2,1,0:T(8,128)S(1)} %get-tuple-element.87), channel_id=1, source_target_pairs={{0,4},{4,8},{8,12},{12,0},{1,5},{5,9},{9,13},{13,1},{2,6},{6,10},{... | collective-permute-start | bytes 9224 | tf_op jit(solution)/shard_map/ppermute | solution.py:21
  221.8 12.5 %collective-permute-start.22 = (f32[1,3,16,16,1]{4,3,2,1,0:T(8,128)S(1)}, f32[1,3,16,16,1]{4,3,2,1,0:T(8,128)S(1)}, u32[]{:S(2)}, u32[]{:S(2)}) collective-permute-start(f32[1,3,16,16,1]{4,3,2,1,0:T(8,128)S(1)} %get-tuple-element.88), channel_id=1, source_target_pairs={{4,0},{8,4},{12,8},{0,12},{5,1},{9,5},{13,9},{1,13},{6,2},{10,6},{... | collective-permute-start | bytes 9224 | tf_op jit(solution)/shard_map/ppermute | solution.py:23
  234.8 5.4 %collective-permute-start.25 = (f32[1,3,16,1,130]{4,3,2,1,0:T(1,128)S(1)}, f32[1,3,16,1,130]{4,3,2,1,0:T(1,128)S(1)}, u32[]{:S(2)}, u32[]{:S(2)}) collective-permute-start(f32[1,3,16,1,130]{4,3,2,1,0:T(1,128)S(1)} %get-tuple-element.44), channel_id=1, source_target_pairs={{0,1},{1,2},{2,3},{3,0},{4,5},{5,6},{6,7},{7,4},{8,9},{9,10},{10,1... | collective-permute-start | bytes 74888 | tf_op jit(solution)/shard_map/ppermute | solution.py:21
  241.9 12.7 %collective-permute-start.27 = (f32[1,3,16,16,1]{4,3,2,1,0:T(8,128)S(1)}, f32[1,3,16,16,1]{4,3,2,1,0:T(8,128)S(1)}, u32[]{:S(2)}, u32[]{:S(2)}) collective-permute-start(f32[1,3,16,16,1]{4,3,2,1,0:T(8,128)S(1)} %get-tuple-element.81), channel_id=1, source_target_pairs={{0,4},{4,8},{8,12},{12,0},{1,5},{5,9},{9,13},{13,1},{2,6},{6,10},{... | collective-permute-start | bytes 9224 | tf_op jit(solution)/shard_map/ppermute | solution.py:21
  242.0 12.6 %collective-permute-start.26 = (f32[1,3,16,16,1]{4,3,2,1,0:T(8,128)S(1)}, f32[1,3,16,16,1]{4,3,2,1,0:T(8,128)S(1)}, u32[]{:S(2)}, u32[]{:S(2)}) collective-permute-start(f32[1,3,16,16,1]{4,3,2,1,0:T(8,128)S(1)} %get-tuple-element.82), channel_id=1, source_target_pairs={{4,0},{8,4},{12,8},{0,12},{5,1},{9,5},{13,9},{1,13},{6,2},{10,6},{... | collective-permute-start | bytes 9224 | tf_op jit(solution)/shard_map/ppermute | solution.py:23
  261.9 12.8 %collective-permute-start.31 = (f32[1,3,16,16,1]{4,3,2,1,0:T(8,128)S(1)}, f32[1,3,16,16,1]{4,3,2,1,0:T(8,128)S(1)}, u32[]{:S(2)}, u32[]{:S(2)}) collective-permute-start(f32[1,3,16,16,1]{4,3,2,1,0:T(8,128)S(1)} %get-tuple-element.75), channel_id=1, source_target_pairs={{0,4},{4,8},{8,12},{12,0},{1,5},{5,9},{9,13},{13,1},{2,6},{6,10},{... | collective-permute-start | bytes 9224 | tf_op jit(solution)/shard_map/ppermute | solution.py:21
  262.0 12.7 %collective-permute-start.30 = (f32[1,3,16,16,1]{4,3,2,1,0:T(8,128)S(1)}, f32[1,3,16,16,1]{4,3,2,1,0:T(8,128)S(1)}, u32[]{:S(2)}, u32[]{:S(2)}) collective-permute-start(f32[1,3,16,16,1]{4,3,2,1,0:T(8,128)S(1)} %get-tuple-element.76), channel_id=1, source_target_pairs={{4,0},{8,4},{12,8},{0,12},{5,1},{9,5},{13,9},{1,13},{6,2},{10,6},{... | collective-permute-start | bytes 9224 | tf_op jit(solution)/shard_map/ppermute | solution.py:23
  (11 other events, 146.0 us)
where the time goes:
time: 288 us; the launch traced here: 283 us
  waiting for transfers between devices  103 us (36%)
  blocking collectives  70.6 us (25%)
  starting transfers between devices  62.2 us (22%)
  other arithmetic  28.9 us (10%)
  local copies, waits for them, and re-layouts  11.6 us (4%)
  between operations  7.19 us (2%)
    ppermute x17, waiting for transfers between devices, padded_2(): lax.ppermute(tail, axis, [(i, (i + 1) % count) for i in range(ends)])  88.4 us
    psum x1, blocking collectives, body(): summed = lax.psum(partial_value, ('gx', 'gy'))  37.7 us
    ppermute x17, starting transfers between devices, padded_2(): lax.ppermute(head, axis, [((i + 1) % count, i) for i in range(ends)])  33.8 us
    unnamed x1, blocking collectives  32.9 us
    ppermute x17, starting transfers between devices, padded_2(): lax.ppermute(tail, axis, [(i, (i + 1) % count) for i in range(ends)])  28.4 us
    ppermute x17, waiting for transfers between devices, padded_2(): lax.ppermute(head, axis, [((i + 1) % count, i) for i in range(ends)])  14.4 us
    another operation x16, other arithmetic, torque_rate(): jnp.stack([scale * (cx + damp * dx), scale * (cy + damp * dy), scale * (c...  11.6 us
  transfers between devices with their start and end apart: 34, of which 23 were waited for; matrix products, arithmetic and copies ran while one was open for 5% of the time, Pallas kernels for 0%

commit v1 on v0

v1 whole, which is shorter than its diff:
```python
import jax
import jax.numpy as jnp
from jax import lax
from jax.experimental import pallas as pl
from jax.experimental.pallas import tpu as pltpu
from jax.sharding import PartitionSpec as P

STEPS = 4
EPS = 1e-06
TIME_STEP = 0.05
REGIONS = 8

ROWS = 16
RIM = 8
EXT = ROWS + 2 * RIM
HALF = ROWS // 2
LANES = 128
Y_LO = 2
MESH = pl.DeviceIdType.MESH


def roll_lanes(x, shift):
    shift = shift % LANES
    return x if shift == 0 else pltpu.roll(x, shift, axis=1)


def kernel(
    shape,
    mag, regions, lower, weights, anisotropy, damping,
    out,
    own, below, above, partner, reg,
    pack_own, pack_partner, rim_own, rim_partner, rim_start,
    main, main_next, main_coef, strip, strip_next, strip_coef, result,
    red_src, red_buf, line_src, line_buf,
    load_sem, out_sem, send_sem, recv_sem, red_sem,
):
    n_img, n_gx, n_gy = shape
    n_z = n_img // Y_LO
    img, gx, gy = lax.axis_index("img"), lax.axis_index("gx"), lax.axis_index("gy")
    y_lo, z = img // n_z, img % n_z
    left, right = lax.rem(gx + n_gx - 1, n_gx), lax.rem(gx + 1, n_gx)
    back, front = lax.rem(gy + n_gy - 1, n_gy), lax.rem(gy + 1, n_gy)
    prev, nxt = lax.rem(img + n_img - 1, n_img), lax.rem(img + 1, n_img)

    plane = Y_LO * n_gx * n_gy
    me_plane = (y_lo * n_gx + gx) * n_gy + gy

    def plane_peer(d):
        t = lax.rem(me_plane + d, plane)
        return ((t // (n_gx * n_gy)) * n_z + z, (t // n_gy) % n_gx, t % n_gy)

    def line_peer(d):
        return (y_lo * n_z + lax.rem(z + d, n_z), gx, gy)

    barrier = pltpu.get_barrier_semaphore()
    peers = [(prev, gx, gy), (nxt, gx, gy)]
    peers += [plane_peer(d) for d in range(1, plane)]
    peers += [line_peer(d) for d in range(1, n_z)]
    for peer in peers:
        pl.semaphore_signal(barrier, inc=1, device_id=peer, device_id_type=MESH)

    for y in range(ROWS):
        for h in range(2):
            pltpu.make_async_copy(
                mag.at[:, :, h, y, 0, :], own.at[RIM + y, h], load_sem.at[0]
            ).start()
            pltpu.make_async_copy(
                regions.at[:, h, y, 0, :], reg.at[RIM + y, h], load_sem.at[1]
            ).start()
    inner = pl.ds(RIM, ROWS)
    pltpu.make_async_copy(own.at[inner], own.at[inner], load_sem.at[0]).wait()
    pltpu.make_async_copy(reg.at[inner], reg.at[inner], load_sem.at[1]).wait()

    lane = lax.broadcasted_iota(jnp.int32, (8, LANES), 1)
    sub = lax.broadcasted_iota(jnp.int32, (8, LANES), 0)
    group = lane // RIM

    def packed(load, half, side):
        total = None
        for h in range(2):
            for k in range(8):
                at = h * 64 + k * 8
                piece = roll_lanes(load(RIM + half * 8 + k, h), at + (0 if side == 0 else RIM))
                total = piece if total is None else jnp.where(group == h * 8 + k, piece, total)
        return total

    for half in range(2):
        for side in range(2):
            for c in range(3):
                pack_own[side, half, c] = packed(lambda r, h: own[r, h, c], half, side)
            pack_own[side, half, 3] = packed(
                lambda r, h: reg[r, h].astype(jnp.float32), half, side
            )

    pl.semaphore_wait(barrier, len(peers))

    copies = []

    def send(src, dst, peer):
        n = len(copies)
        copy = pltpu.make_async_remote_copy(
            src_ref=src, dst_ref=dst, send_sem=send_sem.at[n], recv_sem=recv_sem.at[n],
            device_id=peer, device_id_type=MESH,
        )
        copy.start()
        copies.append(copy)
        return copy

    def send_rims(field, pack, rim):
        got = [
            send(field.at[pl.ds(RIM, RIM)], field.at[pl.ds(RIM + ROWS, RIM)], (img, gx, back)),
            send(field.at[pl.ds(RIM + HALF, RIM)], field.at[pl.ds(0, RIM)], (img, gx, front)),
            send(pack.at[1], rim.at[0, pl.ds(1, 2)], (img, right, gy)),
            send(pack.at[0], rim.at[1, pl.ds(1, 2)], (img, left, gy)),
            send(pack.at[1, 1], rim.at[0, 0], (img, right, front)),
            send(pack.at[1, 0], rim.at[0, 3], (img, right, back)),
            send(pack.at[0, 1], rim.at[1, 0], (img, left, front)),
            send(pack.at[0, 0], rim.at[1, 3], (img, left, back)),
        ]
        return got

    low, high = pl.ds(0, HALF), pl.ds(HALF, HALF)
    own_low, own_high = pl.ds(RIM, HALF), pl.ds(RIM + HALF, HALF)
    early = [
        send(own.at[own_low], below.at[low], (nxt, gx, gy)),
        send(own.at[own_high], above.at[high], (prev, gx, gy)),
    ]
    late = [
        send(own.at[own_high], below.at[high], (nxt, gx, gy)),
        send(own.at[own_low], above.at[low], (prev, gx, gy)),
    ]
    own_rims = send_rims(own, pack_own, rim_own)
    reg_rims = [
        send(reg.at[pl.ds(RIM, RIM)], reg.at[pl.ds(RIM + ROWS, RIM)], (img, gx, back)),
        send(reg.at[pl.ds(RIM + HALF, RIM)], reg.at[pl.ds(0, RIM)], (img, gx, front)),
    ]

    for copy in early:
        copy.wait_recv()

    def add_squares(r, sums):
        first, second = sums
        for h in range(2):
            for c in range(3):
                d = own[RIM + r, h, c] - below[r, h, c]
                first = first + d * d
                d = own[RIM + HALF + r, h, c] - above[HALF + r, h, c]
                second = second + d * d
        return first, second

    zero = jnp.zeros((8, LANES), jnp.float32)
    first, second = lax.fori_loop(0, HALF, add_squares, (zero, zero))
    row_lane = lax.broadcasted_iota(jnp.int32, (1, LANES), 1)
    partial = jnp.where(row_lane == img, jnp.sum(first), 0.0)
    partial = partial + jnp.where(row_lane == img + 1, jnp.sum(second), 0.0)
    red_src[...] = partial
    for d in range(1, plane):
        pltpu.make_async_remote_copy(
            src_ref=red_src, dst_ref=red_buf.at[d - 1], send_sem=red_sem.at[0],
            recv_sem=red_sem.at[1], device_id=plane_peer(d), device_id_type=MESH,
        ).start()

    for copy in late:
        copy.wait_recv()
    low_image = lower[img]
    use_above = jnp.full((8, LANES), low_image, jnp.int32) == img

    def choose(r, carry):
        for h in range(2):
            for c in range(3):
                partner[RIM + r, h, c] = jnp.where(use_above, above[r, h, c], below[r, h, c])
        return carry

    lax.fori_loop(0, ROWS, choose, 0)
    for half in range(2):
        for side in range(2):
            for c in range(3):
                pack_partner[side, half, c] = packed(
                    lambda r, h: partner[r, h, c], half, side
                )
    partner_rims = send_rims(partner, pack_partner, rim_partner)

    whole = pltpu.make_async_remote_copy(
        src_ref=red_buf, dst_ref=red_buf, send_sem=red_sem.at[0], recv_sem=red_sem.at[1],
        device_id=plane_peer(1), device_id_type=MESH,
    )
    whole.wait_recv()
    line_src[...] = red_src[...] + jnp.sum(red_buf[...], axis=0)
    for d in range(1, n_z):
        pltpu.make_async_remote_copy(
            src_ref=line_src, dst_ref=line_buf.at[d - 1], send_sem=red_sem.at[2],
            recv_sem=red_sem.at[3], device_id=line_peer(d), device_id_type=MESH,
        ).start()

    def assembled(i, k, h, load, load_rim, upper):
        at_a, at_b = h * 64 + k * 8, h * 64 + (7 - k) * 8
        group_a, group_b = (0, 3) if upper else (1, 2)
        a, b = load(i, h), load(EXT - 1 - i, h)
        v = roll_lanes(load_rim(1, group_b), 120 - at_b)
        v = jnp.where(lane < 120, roll_lanes(b, 120), v)
        v = jnp.where(lane < 96, roll_lanes(b, 72), v)
        v = jnp.where(lane < 72, roll_lanes(load_rim(0, group_b), 64 - at_b), v)
        v = jnp.where(lane < 64, roll_lanes(load_rim(1, group_a), 56 - at_a), v)
        v = jnp.where(lane < 56, roll_lanes(a, 56), v)
        v = jnp.where(lane < 32, roll_lanes(a, 8), v)
        return jnp.where(lane < 8, roll_lanes(load_rim(0, group_a), -at_a), v)

    def put_coef(ref, i, h, region):
        aniso = jnp.zeros((8, LANES), jnp.float32)
        damp = jnp.zeros((8, LANES), jnp.float32)
        for n in range(REGIONS):
            inside = region == n
            aniso = jnp.where(inside, anisotropy[n], aniso)
            damp = jnp.where(inside, damping[n], damp)
        ref[i, h, 0] = 2.0 * aniso
        ref[i, h, 1] = damp
        ref[i, h, 2] = -TIME_STEP / (1.0 + damp * damp)

    for copy in own_rims + reg_rims:
        copy.wait_recv()

    def main_coefs(r, carry):
        for h in range(2):
            put_coef(main_coef, r, h, reg[r, h])
        return carry

    lax.fori_loop(0, EXT, main_coefs, 0)
    for i in range(ROWS):
        for h in range(2):
            region = assembled(
                i, i % 8, h,
                lambda r, h: reg[r, h].astype(jnp.float32),
                lambda side, g: rim_own[side, g, 3],
                i < 8,
            )
            put_coef(strip_coef, i, h, region.astype(jnp.int32))

    share = jnp.float32(0.0)
    share_all = jnp.float32(0.0)
    for n in range(n_img - 1):
        share = share + jnp.where(n < img, weights[n], 0.0)
        share_all = share_all + weights[n]

    whole_line = pltpu.make_async_remote_copy(
        src_ref=line_buf, dst_ref=line_buf, send_sem=red_sem.at[2], recv_sem=red_sem.at[3],
        device_id=line_peer(1), device_id_type=MESH,
    )
    whole_line.wait_recv()
    squares = line_src[...] + jnp.sum(line_buf[...], axis=0)
    lengths = jnp.where(
        (row_lane >= 1) & (row_lane < n_img), jnp.sqrt(squares + EPS), 0.0
    )
    total = jnp.sum(lengths, axis=1, keepdims=True)
    low_row = jnp.full((1, LANES), low_image, jnp.int32)
    here = jnp.sum(jnp.where(row_lane <= low_row, lengths, 0.0), axis=1, keepdims=True)
    gap = jnp.sum(jnp.where(row_lane == low_row + 1, lengths, 0.0), axis=1, keepdims=True)
    aim = jnp.full((1, 1), share, jnp.float32) / jnp.full((1, 1), share_all, jnp.float32)
    weight = jnp.clip((aim * total - here) / gap, -0.5, 1.5)
    weight = jnp.broadcast_to(weight, (8, LANES))
    own_part = jnp.where(use_above, 1.0 - weight, weight)
    partner_part = jnp.where(use_above, weight, 1.0 - weight)

    def unit(v):
        scale = lax.rsqrt(v[0] * v[0] + v[1] * v[1] + v[2] * v[2])
        return [x * scale for x in v]

    for copy in partner_rims:
        copy.wait_recv()

    def start_main(r, carry):
        for h in range(2):
            v = unit([own_part * own[r, h, c] + partner_part * partner[r, h, c] for c in range(3)])
            for c in range(3):
                main[r, h, c] = v[c]
        return carry

    lax.fori_loop(0, EXT, start_main, 0)
    for side in range(2):
        for g in range(4):
            v = unit([
                own_part * rim_own[side, g, c] + partner_part * rim_partner[side, g, c]
                for c in range(3)
            ])
            for c in range(3):
                rim_start[side, g, c] = v[c]
    for i in range(ROWS):
        for h in range(2):
            for c in range(3):
                strip[i, h, c] = assembled(
                    i, i % 8, h,
                    lambda r, h: main[r, h, c],
                    lambda side, g: rim_start[side, g, c],
                    i < 8,
                )

    def fold(ref):
        for h in range(2):
            for c in range(3):
                ref[ROWS, h, c] = roll_lanes(ref[ROWS - 1, h, c], 64)

    fold(strip)

    first_z, last_z = sub == 0, sub == 7

    def moved(field, coef, r):
        m = [[field[r, h, c] for c in range(3)] for h in range(2)]
        moves = []
        for h in range(2):
            lap = []
            for c in range(3):
                here, other = m[h][c], m[1 - h][c]
                if h == 0:
                    edge = jnp.where(first_z, here, pltpu.roll(other, 1, axis=0))
                else:
                    edge = jnp.where(last_z, here, pltpu.roll(other, 7, axis=0))
                near = roll_lanes(here, 1) + roll_lanes(here, LANES - 1)
                near = near + (field[r - 1, h, c] + field[r + 1, h, c])
                lap.append(near + (other + edge) - 6.0 * here)
            mx, my, mz = m[h]
            twice_aniso, damp, scale = coef[r, h, 0], coef[r, h, 1], coef[r, h, 2]
            hx, hy, hz = lap[0], lap[1], lap[2] + twice_aniso * mz
            gx_ = hx + damp * (my * hz - mz * hy)
            gy_ = hy + damp * (mz * hx - mx * hz)
            gz_ = hz + damp * (mx * hy - my * hx)
            moves.append([
                scale * (my * gz_ - mz * gy_),
                scale * (mz * gx_ - mx * gz_),
                scale * (mx * gy_ - my * gx_),
            ])
        return m, moves

    def predict(field, nextf, coef, r):
        m, moves = moved(field, coef, r)
        for h in range(2):
            for c in range(3):
                nextf[r, h, c] = m[h][c] + moves[h][c]

    def correct(field, nextf, coef, r):
        p, moves = moved(nextf, coef, r)
        new = []
        for h in range(2):
            new.append(unit([(field[r, h, c] + p[h][c]) + moves[h][c] for c in range(3)]))
        return new

    def run(lo, hi, fn):
        def step(r, carry):
            fn(r)
            return carry

        lax.fori_loop(lo, hi, step, 0)

    def correct_to(field, nextf, coef):
        def fn(r):
            new = correct(field, nextf, coef, r)
            for h in range(2):
                for c in range(3):
                    field[r, h, c] = new[h][c]

        return fn

    for step in range(STEPS):
        k = 2 * step + 1
        run(k, EXT - k, lambda r: predict(main, main_next, main_coef, r))
        run(k, ROWS, lambda r: predict(strip, strip_next, strip_coef, r))
        fold(strip_next)
        k = k + 1
        run(k, ROWS, correct_to(strip, strip_next, strip_coef))
        if step < STEPS - 1:
            fold(strip)
            run(k, EXT - k, correct_to(main, main_next, main_coef))

    def finish(base, strip_row):
        def fn(r):
            new = correct(main, main_next, main_coef, r)
            for h in range(2):
                for c in range(3):
                    s = strip[strip_row(r), h, c]
                    v = jnp.where(lane < 8, roll_lanes(s, -(base + 8)), new[h][c])
                    v = jnp.where(lane >= 120, roll_lanes(s, 72 - base), v)
                    result[r - RIM, h, c] = v

        return fn

    run(RIM, ROWS, finish(0, lambda r: r))
    run(ROWS, EXT - RIM, finish(64, lambda r: EXT - 1 - r))
    for y in range(ROWS):
        for h in range(2):
            pltpu.make_async_copy(
                result.at[y, h], out.at[:, :, h, y, 0, :], out_sem
            ).start()
    for copy in copies:
        copy.wait_send()
    whole.wait_send()
    whole_line.wait_send()
    pltpu.make_async_copy(result, result, out_sem).wait()


def body(shape, magnetization, lower_image, image_weights, regions, anisotropy, damping):
    n_img, n_gx, n_gy = shape
    plane = Y_LO * n_gx * n_gy
    f32 = jnp.float32
    tile = (8, LANES)
    smem = pl.BlockSpec(memory_space=pltpu.SMEM)
    anywhere = pl.BlockSpec(memory_space=pl.ANY)
    n_copies = 4 + 8 + 2 + 8
    out = pl.pallas_call(
        lambda *refs: kernel(shape, *refs),
        out_shape=jax.ShapeDtypeStruct((3, 8, 2, ROWS, 1, LANES), f32),
        in_specs=[anywhere, anywhere, smem, smem, smem, smem],
        out_specs=anywhere,
        scratch_shapes=[
            pltpu.VMEM((EXT, 2, 3) + tile, f32),
            pltpu.VMEM((ROWS, 2, 3) + tile, f32),
            pltpu.VMEM((ROWS, 2, 3) + tile, f32),
            pltpu.VMEM((EXT, 2, 3) + tile, f32),
            pltpu.VMEM((EXT, 2) + tile, jnp.int32),
            pltpu.VMEM((2, 2, 4) + tile, f32),
            pltpu.VMEM((2, 2, 3) + tile, f32),
            pltpu.VMEM((2, 4, 4) + tile, f32),
            pltpu.VMEM((2, 4, 3) + tile, f32),
            pltpu.VMEM((2, 4, 3) + tile, f32),
            pltpu.VMEM((EXT, 2, 3) + tile, f32),
            pltpu.VMEM((EXT, 2, 3) + tile, f32),
            pltpu.VMEM((EXT, 2, 3) + tile, f32),
            pltpu.VMEM((ROWS + 1, 2, 3) + tile, f32),
            pltpu.VMEM((ROWS + 1, 2, 3) + tile, f32),
            pltpu.VMEM((ROWS, 2, 3) + tile, f32),
            pltpu.VMEM((ROWS, 2, 3) + tile, f32),
            pltpu.VMEM((1, LANES), f32),
            pltpu.VMEM((plane - 1, 1, LANES), f32),
            pltpu.VMEM((1, LANES), f32),
            pltpu.VMEM((n_img // Y_LO - 1, 1, LANES), f32),
            pltpu.SemaphoreType.DMA((2,)),
            pltpu.SemaphoreType.DMA,
            pltpu.SemaphoreType.DMA((n_copies,)),
            pltpu.SemaphoreType.DMA((n_copies,)),
            pltpu.SemaphoreType.DMA((4,)),
        ],
        compiler_params=pltpu.CompilerParams(collective_id=0, has_side_effects=True),
    )(
        magnetization.reshape(3, 8, 2, ROWS, 1, LANES),
        regions.reshape(8, 2, ROWS, 1, LANES),
        lower_image,
        image_weights,
        anisotropy,
        damping,
    )
    return out.reshape(magnetization.shape)


def solution(mesh):
    placed = (P("img", None, None, "gy", "gx"), P(), P(), P(None, "gy", "gx"), P(), P())
    shape = (mesh.shape["img"], mesh.shape["gx"], mesh.shape["gy"])
    return jax.shard_map(
        lambda *args: body(shape, *args),
        mesh=mesh,
        in_specs=placed,
        out_specs=P("img", None, None, "gy", "gx"),
        check_vma=False,
    )
```

time: 288 us -> 64 us (0.22)
  the two profiles are of different devices: /device:TPU:8 before, /device:TPU:1 now
where the time goes in v1:
time: 64 us; the launch traced here: 63.8 us
  Pallas kernels  62 us (97%)
  local copies, waits for them, and re-layouts  1.77 us (3%)
    pallas_call x1, Pallas kernels, body(): pl.pallas_call(lambda *refs: kernel(shape, *refs), out_shape=jax.ShapeDty...  62 us
    unnamed x1, local copies, waits for them, and re-layouts  1.77 us

profile of v1, /device:TPU:1, one launch (start us, length us, event | category | flops | bytes accessed | tf_op | source)
XLA Modules:
  0.0 63.8 jit_solution(5251822192832807329)
XLA Ops:
  0.0 62.0 %shard_map.64 = f32[3,8,2,16,1,128]{5,4,3,2,1,0:T(1,128)} custom-call(f32[3,8,2,16,1,128]{5,4,3,2,1,0:T(1,128)} %bitcast.4, s32[8,2,16,1,128]{4,3,2,1,0:T(1,128)} %bitcast.5, s32[16]{0:T(128)} %refs_2_.1, f32[15]{0:T(128)} %refs_3_.1, f32[8]{0:T(128)} %refs_4_.1, f32[8]{0:T(128)} %refs_5_.1), custom_call_target="tpu_custom_call" | custom-call | tf_op jit(solution)/shard_map/pallas_call | solution.py:406
  62.0 1.8 %copy.8 = f32[1,3,16,16,128]{4,3,2,1,0:T(8,128)} copy(f32[1,3,16,16,128]{4,3,2,1,0:T(8,128)} %bitcast.3) | data formatting | bytes 786432

commit v2 on v1

--- a/solution.py
+++ b/solution.py
@@ -347,7 +347,7 @@
             fn(r)
             return carry
 
-        lax.fori_loop(lo, hi, step, 0)
+        lax.fori_loop(lo, hi, step, 0, unroll=4)
 
     def correct_to(field, nextf, coef):
         def fn(r):

time: 64 us -> 48.3 us (0.75)
  Pallas kernels: 62 us -> 46.3 us
    pallas_call x1, Pallas kernels: 62 us -> 46.3 us  [body(): pl.pallas_call(lambda *refs: kernel(shape, *refs), out_shape=jax.ShapeDty...]
where the time goes in v2:
time: 48.3 us; the launch traced here: 48.1 us
  Pallas kernels  46.3 us (96%)
  local copies, waits for them, and re-layouts  1.77 us (4%)
    pallas_call x1, Pallas kernels, body(): pl.pallas_call(lambda *refs: kernel(shape, *refs), out_shape=jax.ShapeDty...  46.3 us
    unnamed x1, local copies, waits for them, and re-layouts  1.77 us

profile of v2, /device:TPU:1, one launch (start us, length us, event | category | flops | bytes accessed | tf_op | source)
XLA Modules:
  0.0 48.1 jit_solution(1818550077544962195)
XLA Ops:
  0.0 46.3 %shard_map.64 = f32[3,8,2,16,1,128]{5,4,3,2,1,0:T(1,128)} custom-call(f32[3,8,2,16,1,128]{5,4,3,2,1,0:T(1,128)} %bitcast.4, s32[8,2,16,1,128]{4,3,2,1,0:T(1,128)} %bitcast.5, s32[16]{0:T(128)} %refs_2_.1, f32[15]{0:T(128)} %refs_3_.1, f32[8]{0:T(128)} %refs_4_.1, f32[8]{0:T(128)} %refs_5_.1), custom_call_target="tpu_custom_call" | custom-call | tf_op jit(solution)/shard_map/pallas_call | solution.py:406
  46.3 1.8 %copy.8 = f32[1,3,16,16,128]{4,3,2,1,0:T(8,128)} copy(f32[1,3,16,16,128]{4,3,2,1,0:T(8,128)} %bitcast.3) | data formatting | bytes 786432

commit v3 on v2

--- a/solution.py
+++ b/solution.py
@@ -30,9 +30,9 @@
     out,
     own, below, above, partner, reg,
     pack_own, pack_partner, rim_own, rim_partner, rim_start,
-    main, main_next, main_coef, strip, strip_next, strip_coef, result,
+    main, main_next, main_coef, strip, strip_next, strip_coef, near, result,
     red_src, red_buf, line_src, line_buf,
-    load_sem, out_sem, send_sem, recv_sem, red_sem,
+    load_sem, out_sem, image_sem, send_sem, recv_sem, red_sem,
 ):
     n_img, n_gx, n_gy = shape
     n_z = n_img // Y_LO
@@ -59,11 +59,35 @@
     for peer in peers:
         pl.semaphore_signal(barrier, inc=1, device_id=peer, device_id_type=MESH)
 
+    pl.semaphore_wait(barrier, len(peers))
+
+    to_next, to_prev = (nxt, gx, gy), (prev, gx, gy)
+
+    def send_image(n, rows, field, peer):
+        for y in rows:
+            for h in range(2):
+                pltpu.make_async_remote_copy(
+                    src_ref=mag.at[:, :, h, y, 0, :], dst_ref=field.at[y, h],
+                    send_sem=image_sem.at[0, n], recv_sem=image_sem.at[1, n],
+                    device_id=peer, device_id_type=MESH,
+                ).start()
+        part = field.at[pl.ds(rows[0], len(rows))]
+        return pltpu.make_async_remote_copy(
+            src_ref=part, dst_ref=part, send_sem=image_sem.at[0, n],
+            recv_sem=image_sem.at[1, n], device_id=peer, device_id_type=MESH,
+        )
+
+    low_rows, high_rows = list(range(HALF)), list(range(HALF, ROWS))
+    early = [send_image(0, low_rows, below, to_next), send_image(1, high_rows, above, to_prev)]
+
     for y in range(ROWS):
         for h in range(2):
             pltpu.make_async_copy(
                 mag.at[:, :, h, y, 0, :], own.at[RIM + y, h], load_sem.at[0]
             ).start()
+    late = [send_image(2, high_rows, below, to_next), send_image(3, low_rows, above, to_prev)]
+    for y in range(ROWS):
+        for h in range(2):
             pltpu.make_async_copy(
                 regions.at[:, h, y, 0, :], reg.at[RIM + y, h], load_sem.at[1]
             ).start()
@@ -91,8 +115,6 @@
             pack_own[side, half, 3] = packed(
                 lambda r, h: reg[r, h].astype(jnp.float32), half, side
             )
-
-    pl.semaphore_wait(barrier, len(peers))
 
     copies = []
 
@@ -119,16 +141,6 @@
         ]
         return got
 
-    low, high = pl.ds(0, HALF), pl.ds(HALF, HALF)
-    own_low, own_high = pl.ds(RIM, HALF), pl.ds(RIM + HALF, HALF)
-    early = [
-        send(own.at[own_low], below.at[low], (nxt, gx, gy)),
-        send(own.at[own_high], above.at[high], (prev, gx, gy)),
-    ]
-    late = [
-        send(own.at[own_high], below.at[high], (nxt, gx, gy)),
-        send(own.at[own_low], above.at[low], (prev, gx, gy)),
-    ]
     own_rims = send_rims(own, pack_own, rim_own)
     reg_rims = [
         send(reg.at[pl.ds(RIM, RIM)], reg.at[pl.ds(RIM + ROWS, RIM)], (img, gx, back)),
@@ -212,7 +224,7 @@
             inside = region == n
             aniso = jnp.where(inside, anisotropy[n], aniso)
             damp = jnp.where(inside, damping[n], damp)
-        ref[i, h, 0] = 2.0 * aniso
+        ref[i, h, 0] = 2.0 * aniso - 6.0
         ref[i, h, 1] = damp
         ref[i, h, 2] = -TIME_STEP / (1.0 + damp * damp)
 
@@ -302,8 +314,21 @@
 
     first_z, last_z = sub == 0, sub == 7
 
-    def moved(field, coef, r):
-        m = [[field[r, h, c] for c in range(3)] for h in range(2)]
+    def rows_of(fields, i):
+        tile, edge = fields
+        return [(tile, i), (tile, EXT - 1 - i), (edge, i)]
+
+    def sum_near(fields, i):
+        for n, (ref, r) in enumerate(rows_of(fields, i)):
+            for h in range(2):
+                for c in range(3):
+                    v = ref[r, h, c]
+                    near[i, n, h, c] = roll_lanes(v, 1) + roll_lanes(v, LANES - 1)
+
+    def moved(ref, coef, r, side_sum):
+        rows = ref.at[pl.ds(r - 1, 3)]
+        coefs = coef.at[r]
+        m = [[rows[1, h, c] for c in range(3)] for h in range(2)]
         moves = []
         for h in range(2):
             lap = []
@@ -313,12 +338,11 @@
                     edge = jnp.where(first_z, here, pltpu.roll(other, 1, axis=0))
                 else:
                     edge = jnp.where(last_z, here, pltpu.roll(other, 7, axis=0))
-                near = roll_lanes(here, 1) + roll_lanes(here, LANES - 1)
-                near = near + (field[r - 1, h, c] + field[r + 1, h, c])
-                lap.append(near + (other + edge) - 6.0 * here)
+                beside = rows[0, h, c] + rows[2, h, c]
+                lap.append((beside + (other + edge)) + side_sum[h, c])
             mx, my, mz = m[h]
-            twice_aniso, damp, scale = coef[r, h, 0], coef[r, h, 1], coef[r, h, 2]
-            hx, hy, hz = lap[0], lap[1], lap[2] + twice_aniso * mz
+            hx, hy, hz = lap[0] - 6.0 * mx, lap[1] - 6.0 * my, lap[2] + coefs[h, 0] * mz
+            damp, scale = coefs[h, 1], coefs[h, 2]
             gx_ = hx + damp * (my * hz - mz * hy)
             gy_ = hy + damp * (mz * hx - mx * hz)
             gz_ = hz + damp * (mx * hy - my * hx)
@@ -329,66 +353,58 @@
             ])
         return m, moves
 
-    def predict(field, nextf, coef, r):
-        m, moves = moved(field, coef, r)
-        for h in range(2):
-            for c in range(3):
-                nextf[r, h, c] = m[h][c] + moves[h][c]
-
-    def correct(field, nextf, coef, r):
-        p, moves = moved(nextf, coef, r)
-        new = []
-        for h in range(2):
-            new.append(unit([(field[r, h, c] + p[h][c]) + moves[h][c] for c in range(3)]))
-        return new
-
-    def run(lo, hi, fn):
-        def step(r, carry):
-            fn(r)
+    def evaluate(k, source, base, finish):
+        coefs = (main_coef, strip_coef)
+        sum_near(source, k)
+
+        def step(i, carry):
+            sum_near(source, i + 1)
+            new = []
+            for n, (ref, r) in enumerate(rows_of(source, i)):
+                m, moves = moved(ref, coefs[n // 2], r, near.at[i, n])
+                old = None if base is None else base[n // 2].at[r]
+                for h in range(2):
+                    if old is None:
+                        v = [m[h][c] + moves[h][c] for c in range(3)]
+                    else:
+                        v = unit([(old[h, c] + m[h][c]) + moves[h][c] for c in range(3)])
+                    new.append(v)
+            finish(i, new)
             return carry
 
-        lax.fori_loop(lo, hi, step, 0, unroll=4)
-
-    def correct_to(field, nextf, coef):
-        def fn(r):
-            new = correct(field, nextf, coef, r)
+        lax.fori_loop(k, ROWS, step, 0)
+
+    def store_to(fields):
+        def finish(i, new):
+            for n, (ref, r) in enumerate(rows_of(fields, i)):
+                for h in range(2):
+                    for c in range(3):
+                        ref[r, h, c] = new[2 * n + h][c]
+
+        return finish
+
+    def give_out(i, new):
+        for n, y in enumerate((i - RIM, EXT - 1 - RIM - i)):
             for h in range(2):
                 for c in range(3):
-                    field[r, h, c] = new[h][c]
-
-        return fn
-
+                    s = new[4 + h][c]
+                    v = jnp.where(lane < 8, roll_lanes(s, -(64 * n + 8)), new[2 * n + h][c])
+                    v = jnp.where(lane >= 120, roll_lanes(s, 72 - 64 * n), v)
+                    result[y, h, c] = v
+                pltpu.make_async_copy(
+                    result.at[y, h], out.at[:, :, h, y, 0, :], out_sem
+                ).start()
+
+    now, ahead = (main, strip), (main_next, strip_next)
     for step in range(STEPS):
         k = 2 * step + 1
-        run(k, EXT - k, lambda r: predict(main, main_next, main_coef, r))
-        run(k, ROWS, lambda r: predict(strip, strip_next, strip_coef, r))
+        evaluate(k, now, None, store_to(ahead))
         fold(strip_next)
-        k = k + 1
-        run(k, ROWS, correct_to(strip, strip_next, strip_coef))
-        if step < STEPS - 1:
+        last = step == STEPS - 1
+        evaluate(k + 1, ahead, now, give_out if last else store_to(now))
+        if not last:
             fold(strip)
-            run(k, EXT - k, correct_to(main, main_next, main_coef))
-
-    def finish(base, strip_row):
-        def fn(r):
-            new = correct(main, main_next, main_coef, r)
-            for h in range(2):
-                for c in range(3):
-                    s = strip[strip_row(r), h, c]
-                    v = jnp.where(lane < 8, roll_lanes(s, -(base + 8)), new[h][c])
-                    v = jnp.where(lane >= 120, roll_lanes(s, 72 - base), v)
-                    result[r - RIM, h, c] = v
-
-        return fn
-
-    run(RIM, ROWS, finish(0, lambda r: r))
-    run(ROWS, EXT - RIM, finish(64, lambda r: EXT - 1 - r))
-    for y in range(ROWS):
-        for h in range(2):
-            pltpu.make_async_copy(
-                result.at[y, h], out.at[:, :, h, y, 0, :], out_sem
-            ).start()
-    for copy in copies:
+    for copy in copies + early + late:
         copy.wait_send()
     whole.wait_send()
     whole_line.wait_send()
@@ -402,7 +418,7 @@
     tile = (8, LANES)
     smem = pl.BlockSpec(memory_space=pltpu.SMEM)
     anywhere = pl.BlockSpec(memory_space=pl.ANY)
-    n_copies = 4 + 8 + 2 + 8
+    n_copies = 8 + 2 + 8
     out = pl.pallas_call(
         lambda *refs: kernel(shape, *refs),
         out_shape=jax.ShapeDtypeStruct((3, 8, 2, ROWS, 1, LANES), f32),
@@ -425,6 +441,7 @@
             pltpu.VMEM((ROWS + 1, 2, 3) + tile, f32),
             pltpu.VMEM((ROWS + 1, 2, 3) + tile, f32),
             pltpu.VMEM((ROWS, 2, 3) + tile, f32),
+            pltpu.VMEM((ROWS + 1, 3, 2, 3) + tile, f32),
             pltpu.VMEM((ROWS, 2, 3) + tile, f32),
             pltpu.VMEM((1, LANES), f32),
             pltpu.VMEM((plane - 1, 1, LANES), f32),
@@ -432,6 +449,7 @@
             pltpu.VMEM((n_img // Y_LO - 1, 1, LANES), f32),
             pltpu.SemaphoreType.DMA((2,)),
             pltpu.SemaphoreType.DMA,
+            pltpu.SemaphoreType.DMA((2, 4)),
             pltpu.SemaphoreType.DMA((n_copies,)),
             pltpu.SemaphoreType.DMA((n_copies,)),
             pltpu.SemaphoreType.DMA((4,)),

time: 48.3 us -> 47.8 us (0.990)
  Pallas kernels: 46.3 us -> 45.8 us
    pallas_call x1, Pallas kernels: 46.3 us -> 45.8 us  [body(): pl.pallas_call(lambda *refs: kernel(shape, *refs), out_shape=jax.ShapeDty...]
where the time goes in v3:
time: 47.8 us; the launch traced here: 47.6 us
  Pallas kernels  45.8 us (96%)
  local copies, waits for them, and re-layouts  1.77 us (4%)
    pallas_call x1, Pallas kernels, body(): pl.pallas_call(lambda *refs: kernel(shape, *refs), out_shape=jax.ShapeDty...  45.8 us
    unnamed x1, local copies, waits for them, and re-layouts  1.77 us

profile of v3, /device:TPU:1, one launch (start us, length us, event | category | flops | bytes accessed | tf_op | source)
XLA Modules:
  0.0 47.6 jit_solution(17444944299527818296)
XLA Ops:
  0.0 45.8 %shard_map.64 = f32[3,8,2,16,1,128]{5,4,3,2,1,0:T(1,128)} custom-call(f32[3,8,2,16,1,128]{5,4,3,2,1,0:T(1,128)} %bitcast.4, s32[8,2,16,1,128]{4,3,2,1,0:T(1,128)} %bitcast.5, s32[16]{0:T(128)} %refs_2_.1, f32[15]{0:T(128)} %refs_3_.1, f32[8]{0:T(128)} %refs_4_.1, f32[8]{0:T(128)} %refs_5_.1), custom_call_target="tpu_custom_call" | custom-call | tf_op jit(solution)/shard_map/pallas_call | solution.py:422
  45.8 1.8 %copy.8 = f32[1,3,16,16,128]{4,3,2,1,0:T(8,128)} copy(f32[1,3,16,16,128]{4,3,2,1,0:T(8,128)} %bitcast.3) | data formatting | bytes 786432

commit v4 on v3

--- a/solution.py
+++ b/solution.py
@@ -356,9 +356,9 @@
     def evaluate(k, source, base, finish):
         coefs = (main_coef, strip_coef)
         sum_near(source, k)
-
-        def step(i, carry):
-            sum_near(source, i + 1)
+        for i in range(k, ROWS):
+            if i + 1 < ROWS:
+                sum_near(source, i + 1)
             new = []
             for n, (ref, r) in enumerate(rows_of(source, i)):
                 m, moves = moved(ref, coefs[n // 2], r, near.at[i, n])
@@ -370,9 +370,6 @@
                         v = unit([(old[h, c] + m[h][c]) + moves[h][c] for c in range(3)])
                     new.append(v)
             finish(i, new)
-            return carry
-
-        lax.fori_loop(k, ROWS, step, 0)
 
     def store_to(fields):
         def finish(i, new):
@@ -441,7 +438,7 @@
             pltpu.VMEM((ROWS + 1, 2, 3) + tile, f32),
             pltpu.VMEM((ROWS + 1, 2, 3) + tile, f32),
             pltpu.VMEM((ROWS, 2, 3) + tile, f32),
-            pltpu.VMEM((ROWS + 1, 3, 2, 3) + tile, f32),
+            pltpu.VMEM((ROWS, 3, 2, 3) + tile, f32),
             pltpu.VMEM((ROWS, 2, 3) + tile, f32),
             pltpu.VMEM((1, LANES), f32),
             pltpu.VMEM((plane - 1, 1, LANES), f32),

time: 47.8 us -> 41.4 us (0.87)
  Pallas kernels: 45.8 us -> 39.5 us
    pallas_call x1, Pallas kernels: 45.8 us -> 39.5 us  [body(): pl.pallas_call(lambda *refs: kernel(shape, *refs), out_shape=jax.ShapeDty...]
where the time goes in v4:
time: 41.4 us; the launch traced here: 41.2 us
  Pallas kernels  39.5 us (95%)
  local copies, waits for them, and re-layouts  1.77 us (4%)
    pallas_call x1, Pallas kernels, body(): pl.pallas_call(lambda *refs: kernel(shape, *refs), out_shape=jax.ShapeDty...  39.5 us
    unnamed x1, local copies, waits for them, and re-layouts  1.77 us

profile of v4, /device:TPU:1, one launch (start us, length us, event | category | flops | bytes accessed | tf_op | source)
XLA Modules:
  0.0 41.2 jit_solution(16029293153415796364)
XLA Ops:
  0.0 39.5 %shard_map.64 = f32[3,8,2,16,1,128]{5,4,3,2,1,0:T(1,128)} custom-call(f32[3,8,2,16,1,128]{5,4,3,2,1,0:T(1,128)} %bitcast.4, s32[8,2,16,1,128]{4,3,2,1,0:T(1,128)} %bitcast.5, s32[16]{0:T(128)} %refs_2_.1, f32[15]{0:T(128)} %refs_3_.1, f32[8]{0:T(128)} %refs_4_.1, f32[8]{0:T(128)} %refs_5_.1), custom_call_target="tpu_custom_call" | custom-call | tf_op jit(solution)/shard_map/pallas_call | solution.py:419
  39.5 1.8 %copy.8 = f32[1,3,16,16,128]{4,3,2,1,0:T(8,128)} copy(f32[1,3,16,16,128]{4,3,2,1,0:T(8,128)} %bitcast.3) | data formatting | bytes 786432

commit v5 on v4

--- a/solution.py
+++ b/solution.py
@@ -14,6 +14,7 @@
 RIM = 8
 EXT = ROWS + 2 * RIM
 HALF = ROWS // 2
+CHUNKS = 4
 LANES = 128
 Y_LO = 2
 MESH = pl.DeviceIdType.MESH
@@ -24,15 +25,25 @@
     return x if shift == 0 else pltpu.roll(x, shift, axis=1)
 
 
-def kernel(
+def unit(v):
+    scale = lax.rsqrt(v[0] * v[0] + v[1] * v[1] + v[2] * v[2])
+    return [x * scale for x in v]
+
+
+def fold(ref):
+    for h in range(2):
+        for c in range(3):
+            ref[ROWS, h, c] = roll_lanes(ref[ROWS - 1, h, c], 64)
+
+
+def exchange(
     shape,
-    mag, regions, lower, weights, anisotropy, damping,
-    out,
+    mag, regions, lower_in, weights_in, anisotropy_in, damping_in,
+    main, main_coef, strip, strip_coef,
     own, below, above, partner, reg,
-    pack_own, pack_partner, rim_own, rim_partner, rim_start,
-    main, main_next, main_coef, strip, strip_next, strip_coef, near, result,
-    red_src, red_buf, line_src, line_buf,
-    load_sem, out_sem, image_sem, send_sem, recv_sem, red_sem,
+    pack_own, pack_partner, rim_own, rim_partner,
+    own_strip, partner_strip, red_src, red_buf, line_src, line_buf,
+    lower, weights, anisotropy, damping, table_sem, load_sem, image_sem, send_sem, recv_sem, red_sem,
 ):
     n_img, n_gx, n_gy = shape
     n_z = n_img // Y_LO
@@ -59,33 +70,51 @@
     for peer in peers:
         pl.semaphore_signal(barrier, inc=1, device_id=peer, device_id_type=MESH)
 
+    tables = [
+        pltpu.make_async_copy(src, dst, table_sem.at[n])
+        for n, (src, dst) in enumerate((
+            (lower_in, lower), (weights_in, weights),
+            (anisotropy_in, anisotropy), (damping_in, damping),
+        ))
+    ]
+    for copy in tables:
+        copy.start()
     pl.semaphore_wait(barrier, len(peers))
 
     to_next, to_prev = (nxt, gx, gy), (prev, gx, gy)
 
-    def send_image(n, rows, field, peer):
-        for y in rows:
-            for h in range(2):
-                pltpu.make_async_remote_copy(
-                    src_ref=mag.at[:, :, h, y, 0, :], dst_ref=field.at[y, h],
-                    send_sem=image_sem.at[0, n], recv_sem=image_sem.at[1, n],
-                    device_id=peer, device_id_type=MESH,
-                ).start()
-        part = field.at[pl.ds(rows[0], len(rows))]
-        return pltpu.make_async_remote_copy(
-            src_ref=part, dst_ref=part, send_sem=image_sem.at[0, n],
-            recv_sem=image_sem.at[1, n], device_id=peer, device_id_type=MESH,
-        )
+    def send_images(n, next_rows, prev_rows):
+        ways = [(next_rows, below, to_next, n), (prev_rows, above, to_prev, n + 1)]
+        for j in range(len(next_rows)):
+            for rows, field, peer, m in ways:
+                for h in range(2):
+                    pltpu.make_async_remote_copy(
+                        src_ref=mag.at[:, :, h, rows[j], 0, :], dst_ref=field.at[rows[j], h],
+                        send_sem=image_sem.at[0, m], recv_sem=image_sem.at[1, m],
+                        device_id=peer, device_id_type=MESH,
+                    ).start()
+        parts = [(field.at[pl.ds(rows[0], len(rows))], peer, m) for rows, field, peer, m in ways]
+        return [
+            pltpu.make_async_remote_copy(
+                src_ref=part, dst_ref=part, send_sem=image_sem.at[0, m],
+                recv_sem=image_sem.at[1, m], device_id=peer, device_id_type=MESH,
+            )
+            for part, peer, m in parts
+        ]
 
     low_rows, high_rows = list(range(HALF)), list(range(HALF, ROWS))
-    early = [send_image(0, low_rows, below, to_next), send_image(1, high_rows, above, to_prev)]
+    early = send_images(0, low_rows, high_rows)
 
     for y in range(ROWS):
         for h in range(2):
             pltpu.make_async_copy(
                 mag.at[:, :, h, y, 0, :], own.at[RIM + y, h], load_sem.at[0]
             ).start()
-    late = [send_image(2, high_rows, below, to_next), send_image(3, low_rows, above, to_prev)]
+    step = HALF // CHUNKS
+    late = [
+        send_images(2 + 2 * q, high_rows[q * step : (q + 1) * step], low_rows[q * step : (q + 1) * step])
+        for q in range(CHUNKS)
+    ]
     for y in range(ROWS):
         for h in range(2):
             pltpu.make_async_copy(
@@ -128,24 +157,29 @@
         copies.append(copy)
         return copy
 
-    def send_rims(field, pack, rim):
-        got = [
-            send(field.at[pl.ds(RIM, RIM)], field.at[pl.ds(RIM + ROWS, RIM)], (img, gx, back)),
-            send(field.at[pl.ds(RIM + HALF, RIM)], field.at[pl.ds(0, RIM)], (img, gx, front)),
-            send(pack.at[1], rim.at[0, pl.ds(1, 2)], (img, right, gy)),
-            send(pack.at[0], rim.at[1, pl.ds(1, 2)], (img, left, gy)),
+    def send_rows(field, first, count):
+        return [
+            send(
+                field.at[pl.ds(RIM + first, count)], field.at[pl.ds(RIM + ROWS + first, count)],
+                (img, gx, back),
+            ),
+            send(
+                field.at[pl.ds(RIM + HALF + first, count)], field.at[pl.ds(first, count)],
+                (img, gx, front),
+            ),
+        ]
+
+    def send_packs(pack, rim):
+        return [
             send(pack.at[1, 1], rim.at[0, 0], (img, right, front)),
             send(pack.at[1, 0], rim.at[0, 3], (img, right, back)),
             send(pack.at[0, 1], rim.at[1, 0], (img, left, front)),
             send(pack.at[0, 0], rim.at[1, 3], (img, left, back)),
+            send(pack.at[1], rim.at[0, pl.ds(1, 2)], (img, right, gy)),
+            send(pack.at[0], rim.at[1, pl.ds(1, 2)], (img, left, gy)),
         ]
-        return got
-
-    own_rims = send_rims(own, pack_own, rim_own)
-    reg_rims = [
-        send(reg.at[pl.ds(RIM, RIM)], reg.at[pl.ds(RIM + ROWS, RIM)], (img, gx, back)),
-        send(reg.at[pl.ds(RIM + HALF, RIM)], reg.at[pl.ds(0, RIM)], (img, gx, front)),
-    ]
+
+    own_rims = send_packs(pack_own, rim_own) + send_rows(own, 0, RIM) + send_rows(reg, 0, RIM)
 
     for copy in early:
         copy.wait_recv()
@@ -172,25 +206,26 @@
             recv_sem=red_sem.at[1], device_id=plane_peer(d), device_id_type=MESH,
         ).start()
 
-    for copy in late:
-        copy.wait_recv()
+    for copy in tables:
+        copy.wait()
     low_image = lower[img]
     use_above = jnp.full((8, LANES), low_image, jnp.int32) == img
-
-    def choose(r, carry):
-        for h in range(2):
-            for c in range(3):
-                partner[RIM + r, h, c] = jnp.where(use_above, above[r, h, c], below[r, h, c])
-        return carry
-
-    lax.fori_loop(0, ROWS, choose, 0)
+    partner_rims = []
+    for q in range(CHUNKS):
+        for copy in late[q]:
+            copy.wait_recv()
+        for r in low_rows[q * step : (q + 1) * step] + high_rows[q * step : (q + 1) * step]:
+            for h in range(2):
+                for c in range(3):
+                    partner[RIM + r, h, c] = jnp.where(use_above, above[r, h, c], below[r, h, c])
+        partner_rims += send_rows(partner, q * step, step)
     for half in range(2):
         for side in range(2):
             for c in range(3):
                 pack_partner[side, half, c] = packed(
                     lambda r, h: partner[r, h, c], half, side
                 )
-    partner_rims = send_rims(partner, pack_partner, rim_partner)
+    partner_rims += send_packs(pack_partner, rim_partner)
 
     whole = pltpu.make_async_remote_copy(
         src_ref=red_buf, dst_ref=red_buf, send_sem=red_sem.at[0], recv_sem=red_sem.at[1],
@@ -228,7 +263,7 @@
         ref[i, h, 1] = damp
         ref[i, h, 2] = -TIME_STEP / (1.0 + damp * damp)
 
-    for copy in own_rims + reg_rims:
+    for copy in own_rims:
         copy.wait_recv()
 
     def main_coefs(r, carry):
@@ -247,11 +282,26 @@
             )
             put_coef(strip_coef, i, h, region.astype(jnp.int32))
 
+    def assemble(into, field, rim):
+        for i in range(ROWS):
+            for h in range(2):
+                for c in range(3):
+                    into[i, h, c] = assembled(
+                        i, i % 8, h, lambda r, h: field[r, h, c], lambda side, g: rim[side, g, c],
+                        i < 8,
+                    )
+
+    assemble(own_strip, own, rim_own)
+
     share = jnp.float32(0.0)
     share_all = jnp.float32(0.0)
     for n in range(n_img - 1):
         share = share + jnp.where(n < img, weights[n], 0.0)
         share_all = share_all + weights[n]
+
+    for copy in partner_rims:
+        copy.wait_recv()
+    assemble(partner_strip, partner, rim_partner)
 
     whole_line = pltpu.make_async_remote_copy(
         src_ref=line_buf, dst_ref=line_buf, send_sem=red_sem.at[2], recv_sem=red_sem.at[3],
@@ -272,46 +322,34 @@
     own_part = jnp.where(use_above, 1.0 - weight, weight)
     partner_part = jnp.where(use_above, weight, 1.0 - weight)
 
-    def unit(v):
-        scale = lax.rsqrt(v[0] * v[0] + v[1] * v[1] + v[2] * v[2])
-        return [x * scale for x in v]
-
-    for copy in partner_rims:
-        copy.wait_recv()
-
-    def start_main(r, carry):
-        for h in range(2):
-            v = unit([own_part * own[r, h, c] + partner_part * partner[r, h, c] for c in range(3)])
-            for c in range(3):
-                main[r, h, c] = v[c]
-        return carry
-
-    lax.fori_loop(0, EXT, start_main, 0)
-    for side in range(2):
-        for g in range(4):
-            v = unit([
-                own_part * rim_own[side, g, c] + partner_part * rim_partner[side, g, c]
-                for c in range(3)
-            ])
-            for c in range(3):
-                rim_start[side, g, c] = v[c]
-    for i in range(ROWS):
-        for h in range(2):
-            for c in range(3):
-                strip[i, h, c] = assembled(
-                    i, i % 8, h,
-                    lambda r, h: main[r, h, c],
-                    lambda side, g: rim_start[side, g, c],
-                    i < 8,
-                )
-
-    def fold(ref):
-        for h in range(2):
-            for c in range(3):
-                ref[ROWS, h, c] = roll_lanes(ref[ROWS - 1, h, c], 64)
-
+    def start(into, ours, theirs, count):
+        def step(r, carry):
+            for h in range(2):
+                v = unit([
+                    own_part * ours[r, h, c] + partner_part * theirs[r, h, c] for c in range(3)
+                ])
+                for c in range(3):
+                    into[r, h, c] = v[c]
+            return carry
+
+        lax.fori_loop(0, count, step, 0, unroll=8)
+
+    start(strip, own_strip, partner_strip, ROWS)
+    start(main, own, partner, EXT)
     fold(strip)
 
+    for copy in copies + early + sum(late, []):
+        copy.wait_send()
+    whole.wait_send()
+    whole_line.wait_send()
+
+
+def evolve(
+    main_in, main_coef, strip_in, strip_coef, out,
+    main, main_next, strip, strip_next, near, result, out_sem,
+):
+    lane = lax.broadcasted_iota(jnp.int32, (8, LANES), 1)
+    sub = lax.broadcasted_iota(jnp.int32, (8, LANES), 0)
     first_z, last_z = sub == 0, sub == 7
 
     def rows_of(fields, i):
@@ -392,19 +430,16 @@
                     result.at[y, h], out.at[:, :, h, y, 0, :], out_sem
                 ).start()
 
-    now, ahead = (main, strip), (main_next, strip_next)
+    first, now, ahead = (main_in, strip_in), (main, strip), (main_next, strip_next)
     for step in range(STEPS):
         k = 2 * step + 1
-        evaluate(k, now, None, store_to(ahead))
+        base = now if step else first
+        evaluate(k, base, None, store_to(ahead))
         fold(strip_next)
         last = step == STEPS - 1
-        evaluate(k + 1, ahead, now, give_out if last else store_to(now))
+        evaluate(k + 1, ahead, base, give_out if last else store_to(now))
         if not last:
             fold(strip)
-    for copy in copies + early + late:
-        copy.wait_send()
-    whole.wait_send()
-    whole_line.wait_send()
     pltpu.make_async_copy(result, result, out_sem).wait()
 
 
@@ -413,14 +448,15 @@
     plane = Y_LO * n_gx * n_gy
     f32 = jnp.float32
     tile = (8, LANES)
-    smem = pl.BlockSpec(memory_space=pltpu.SMEM)
     anywhere = pl.BlockSpec(memory_space=pl.ANY)
-    n_copies = 8 + 2 + 8
-    out = pl.pallas_call(
-        lambda *refs: kernel(shape, *refs),
-        out_shape=jax.ShapeDtypeStruct((3, 8, 2, ROWS, 1, LANES), f32),
-        in_specs=[anywhere, anywhere, smem, smem, smem, smem],
-        out_specs=anywhere,
+    n_copies = (6 + 2 + 2) + (6 + 2 * CHUNKS)
+    fields = [(EXT, 2, 3) + tile, (EXT, 2, 3) + tile, (ROWS + 1, 2, 3) + tile, (ROWS, 2, 3) + tile]
+    vmem = pl.BlockSpec(memory_space=pltpu.VMEM)
+    parts = pl.pallas_call(
+        lambda *refs: exchange(shape, *refs),
+        out_shape=[pltpu.VMEM(dims, f32) for dims in fields],
+        in_specs=[anywhere] * 6,
+        out_specs=[vmem] * 4,
         scratch_shapes=[
             pltpu.VMEM((EXT, 2, 3) + tile, f32),
             pltpu.VMEM((ROWS, 2, 3) + tile, f32),
@@ -431,22 +467,19 @@
             pltpu.VMEM((2, 2, 3) + tile, f32),
             pltpu.VMEM((2, 4, 4) + tile, f32),
             pltpu.VMEM((2, 4, 3) + tile, f32),
-            pltpu.VMEM((2, 4, 3) + tile, f32),
-            pltpu.VMEM((EXT, 2, 3) + tile, f32),
-            pltpu.VMEM((EXT, 2, 3) + tile, f32),
-            pltpu.VMEM((EXT, 2, 3) + tile, f32),
-            pltpu.VMEM((ROWS + 1, 2, 3) + tile, f32),
-            pltpu.VMEM((ROWS + 1, 2, 3) + tile, f32),
             pltpu.VMEM((ROWS, 2, 3) + tile, f32),
-            pltpu.VMEM((ROWS, 3, 2, 3) + tile, f32),
             pltpu.VMEM((ROWS, 2, 3) + tile, f32),
             pltpu.VMEM((1, LANES), f32),
             pltpu.VMEM((plane - 1, 1, LANES), f32),
             pltpu.VMEM((1, LANES), f32),
             pltpu.VMEM((n_img // Y_LO - 1, 1, LANES), f32),
+            pltpu.SMEM((n_img,), jnp.int32),
+            pltpu.SMEM((n_img - 1,), f32),
+            pltpu.SMEM((REGIONS,), f32),
+            pltpu.SMEM((REGIONS,), f32),
+            pltpu.SemaphoreType.DMA((4,)),
             pltpu.SemaphoreType.DMA((2,)),
-            pltpu.SemaphoreType.DMA,
-            pltpu.SemaphoreType.DMA((2, 4)),
+            pltpu.SemaphoreType.DMA((2, 2 + 2 * CHUNKS)),
             pltpu.SemaphoreType.DMA((n_copies,)),
             pltpu.SemaphoreType.DMA((n_copies,)),
             pltpu.SemaphoreType.DMA((4,)),
@@ -460,6 +493,21 @@
         anisotropy,
         damping,
     )
+    out = pl.pallas_call(
+        evolve,
+        out_shape=jax.ShapeDtypeStruct((3, 8, 2, ROWS, 1, LANES), f32),
+        in_specs=[vmem] * 4,
+        out_specs=anywhere,
+        scratch_shapes=[
+            pltpu.VMEM((EXT, 2, 3) + tile, f32),
+            pltpu.VMEM((EXT, 2, 3) + tile, f32),
+            pltpu.VMEM((ROWS + 1, 2, 3) + tile, f32),
+            pltpu.VMEM((ROWS + 1, 2, 3) + tile, f32),
+            pltpu.VMEM((ROWS, 3, 2, 3) + tile, f32),
+            pltpu.VMEM((ROWS, 2, 3) + tile, f32),
+            pltpu.SemaphoreType.DMA,
+        ],
+    )(*[pltpu.with_memory_space_constraint(p, pltpu.VMEM) for p in parts])
     return out.reshape(magnetization.shape)
 
 

time: 41.4 us -> 36.4 us (0.88)
  Pallas kernels: 39.5 us -> 36.3 us
  local copies, waits for them, and re-layouts: 1.77 us -> 0 us
    pallas_call x1 -> x2, Pallas kernels: 39.5 us -> 36.3 us  [the longest x1 30.3 us: body(): pl.pallas_call(lambda *refs: exchange(shape, *refs), out_shape=[pltpu.VME...]
    unnamed x1 -> x0, local copies, waits for them, and re-layouts: 1.77 us -> none
where the time goes in v5:
time: 36.4 us; the launch traced here: 36.3 us
  Pallas kernels  36.3 us (100%)
    pallas_call x1, Pallas kernels, body(): pl.pallas_call(lambda *refs: exchange(shape, *refs), out_shape=[pltpu.VME...  30.3 us
    pallas_call x1, Pallas kernels, body(): pl.pallas_call(evolve, out_shape=jax.ShapeDtypeStruct((3, 8, 2, ROWS, 1,...  5.92 us

profile of v5, /device:TPU:1, one launch (start us, length us, event | category | flops | bytes accessed | tf_op | source)
XLA Modules:
  0.0 36.3 jit_solution(7888058139860511592)
XLA Ops:
  0.0 30.3 %shard_map.64 = (f32[32,2,3,8,128]{4,3,2,1,0:T(8,128)S(1)}, f32[32,2,3,8,128]{4,3,2,1,0:T(8,128)S(1)}, f32[17,2,3,8,128]{4,3,2,1,0:T(8,128)S(1)}, f32[16,2,3,8,128]{4,3,2,1,0:T(8,128)S(1)}) custom-call(f32[3,8,2,16,1,128]{5,4,3,2,1,0:T(1,128)} %bitcast.3, s32[8,2,16,1,128]{4,3,2,1,0:T(1,128)} %bitcast.4, s32[16]{0:T(128)} %refs_2_.1, f32[15]{0:T(128)} %refs_3_.1, ...), custom_call_target="tpu_custom_call" | custom-call | tf_op jit(solution)/shard_map/pallas_call | solution.py:455
  30.3 5.9 %shard_map.65 = f32[3,8,2,16,1,128]{5,4,3,2,1,0:T(1,128)} custom-call(f32[32,2,3,8,128]{4,3,2,1,0:T(8,128)S(1)} %get-tuple-element.9.main_in, f32[32,2,3,8,128]{4,3,2,1,0:T(8,128)S(1)} %get-tuple-element.10.main_coef, f32[17,2,3,8,128]{4,3,2,1,0:T(8,128)S(1)} %get-tuple-element.11.strip_in, f32[16,2,3,8,128]{4,3,2,1,0:T(8,128)S(1)} %get-tuple-element.12.strip_coef), custom_call_target="tpu_custom_call" | custom-call | tf_op jit(solution)/shard_map/pallas_call | solution.py:496

commit v6 on v5

--- a/solution.py
+++ b/solution.py
@@ -43,7 +43,7 @@
     own, below, above, partner, reg,
     pack_own, pack_partner, rim_own, rim_partner,
     own_strip, partner_strip, red_src, red_buf, line_src, line_buf,
-    lower, weights, anisotropy, damping, table_sem, load_sem, image_sem, send_sem, recv_sem, red_sem,
+    lower, weights, anisotropy, damping, round_sem, table_sem, load_sem, image_sem, send_sem, recv_sem, red_sem,
 ):
     n_img, n_gx, n_gy = shape
     n_z = n_img // Y_LO
@@ -64,11 +64,21 @@
         return (y_lo * n_z + lax.rem(z + d, n_z), gx, gy)
 
     barrier = pltpu.get_barrier_semaphore()
-    peers = [(prev, gx, gy), (nxt, gx, gy)]
-    peers += [plane_peer(d) for d in range(1, plane)]
-    peers += [line_peer(d) for d in range(1, n_z)]
-    for peer in peers:
-        pl.semaphore_signal(barrier, inc=1, device_id=peer, device_id_type=MESH)
+    nearby = [
+        (prev, gx, gy), (nxt, gx, gy),
+        (img, left, gy), (img, right, gy), (img, gx, back), (img, gx, front),
+        (img, left, back), (img, left, front), (img, right, back), (img, right, front),
+        (lax.rem(img + n_z, n_img), gx, gy),
+    ]
+
+    def tell(sem):
+        for peer in nearby:
+            pl.semaphore_signal(sem, inc=1, device_id=peer, device_id_type=MESH)
+
+    def heard(sem):
+        pl.semaphore_wait(sem, len(nearby))
+
+    tell(barrier)
 
     tables = [
         pltpu.make_async_copy(src, dst, table_sem.at[n])
@@ -79,7 +89,7 @@
     ]
     for copy in tables:
         copy.start()
-    pl.semaphore_wait(barrier, len(peers))
+    heard(barrier)
 
     to_next, to_prev = (nxt, gx, gy), (prev, gx, gy)
 
@@ -103,6 +113,7 @@
         ]
 
     low_rows, high_rows = list(range(HALF)), list(range(HALF, ROWS))
+    tell(round_sem.at[0])
     early = send_images(0, low_rows, high_rows)
 
     for y in range(ROWS):
@@ -181,6 +192,9 @@
 
     own_rims = send_packs(pack_own, rim_own) + send_rows(own, 0, RIM) + send_rows(reg, 0, RIM)
 
+    heard(round_sem.at[0])
+    tell(round_sem.at[1])
+
     for copy in early:
         copy.wait_recv()
 
@@ -196,10 +210,14 @@
 
     zero = jnp.zeros((8, LANES), jnp.float32)
     first, second = lax.fori_loop(0, HALF, add_squares, (zero, zero))
+    heard(round_sem.at[1])
+    tell(round_sem.at[2])
     row_lane = lax.broadcasted_iota(jnp.int32, (1, LANES), 1)
-    partial = jnp.where(row_lane == img, jnp.sum(first), 0.0)
-    partial = partial + jnp.where(row_lane == img + 1, jnp.sum(second), 0.0)
-    red_src[...] = partial
+    first, second = (
+        jnp.sum(jnp.sum(v, axis=0, keepdims=True), axis=1, keepdims=True) for v in (first, second)
+    )
+    partial = jnp.where(row_lane == img, first, 0.0)
+    red_src[...] = partial + jnp.where(row_lane == img + 1, second, 0.0)
     for d in range(1, plane):
         pltpu.make_async_remote_copy(
             src_ref=red_src, dst_ref=red_buf.at[d - 1], send_sem=red_sem.at[0],
@@ -232,6 +250,7 @@
         device_id=plane_peer(1), device_id_type=MESH,
     )
     whole.wait_recv()
+    heard(round_sem.at[2])
     line_src[...] = red_src[...] + jnp.sum(red_buf[...], axis=0)
     for d in range(1, n_z):
         pltpu.make_async_remote_copy(
@@ -477,6 +496,7 @@
             pltpu.SMEM((n_img - 1,), f32),
             pltpu.SMEM((REGIONS,), f32),
             pltpu.SMEM((REGIONS,), f32),
+            pltpu.SemaphoreType.REGULAR((3,)),
             pltpu.SemaphoreType.DMA((4,)),
             pltpu.SemaphoreType.DMA((2,)),
             pltpu.SemaphoreType.DMA((2, 2 + 2 * CHUNKS)),

time: 36.4 us -> 35.6 us (0.978)
  Pallas kernels: 36.3 us -> 35.4 us
    pallas_call x1, Pallas kernels: 30.3 us -> 29.5 us  [body(): pl.pallas_call(lambda *refs: exchange(shape, *refs), out_shape=[pltpu.VME...]
where the time goes in v6:
time: 35.6 us; the launch traced here: 35.4 us
  Pallas kernels  35.4 us (99%)
    pallas_call x1, Pallas kernels, body(): pl.pallas_call(lambda *refs: exchange(shape, *refs), out_shape=[pltpu.VME...  29.5 us
    pallas_call x1, Pallas kernels, body(): pl.pallas_call(evolve, out_shape=jax.ShapeDtypeStruct((3, 8, 2, ROWS, 1,...  5.92 us

profile of v6, /device:TPU:1, one launch (start us, length us, event | category | flops | bytes accessed | tf_op | source)
XLA Modules:
  0.0 35.4 jit_solution(5758685898536411006)
XLA Ops:
  0.0 29.5 %shard_map.64 = (f32[32,2,3,8,128]{4,3,2,1,0:T(8,128)S(1)}, f32[32,2,3,8,128]{4,3,2,1,0:T(8,128)S(1)}, f32[17,2,3,8,128]{4,3,2,1,0:T(8,128)S(1)}, f32[16,2,3,8,128]{4,3,2,1,0:T(8,128)S(1)}) custom-call(f32[3,8,2,16,1,128]{5,4,3,2,1,0:T(1,128)} %bitcast.3, s32[8,2,16,1,128]{4,3,2,1,0:T(1,128)} %bitcast.4, s32[16]{0:T(128)} %refs_2_.1, f32[15]{0:T(128)} %refs_3_.1, ...), custom_call_target="tpu_custom_call" | custom-call | tf_op jit(solution)/shard_map/pallas_call | solution.py:474
  29.5 5.9 %shard_map.65 = f32[3,8,2,16,1,128]{5,4,3,2,1,0:T(1,128)} custom-call(f32[32,2,3,8,128]{4,3,2,1,0:T(8,128)S(1)} %get-tuple-element.9.main_in, f32[32,2,3,8,128]{4,3,2,1,0:T(8,128)S(1)} %get-tuple-element.10.main_coef, f32[17,2,3,8,128]{4,3,2,1,0:T(8,128)S(1)} %get-tuple-element.11.strip_in, f32[16,2,3,8,128]{4,3,2,1,0:T(8,128)S(1)} %get-tuple-element.12.strip_coef), custom_call_target="tpu_custom_call" | custom-call | tf_op jit(solution)/shard_map/pallas_call | solution.py:516

commit v7 on v6

--- a/solution.py
+++ b/solution.py
@@ -132,29 +132,24 @@
                 regions.at[:, h, y, 0, :], reg.at[RIM + y, h], load_sem.at[1]
             ).start()
     inner = pl.ds(RIM, ROWS)
-    pltpu.make_async_copy(own.at[inner], own.at[inner], load_sem.at[0]).wait()
-    pltpu.make_async_copy(reg.at[inner], reg.at[inner], load_sem.at[1]).wait()
 
     lane = lax.broadcasted_iota(jnp.int32, (8, LANES), 1)
     sub = lax.broadcasted_iota(jnp.int32, (8, LANES), 0)
     group = lane // RIM
 
-    def packed(load, half, side):
-        total = None
-        for h in range(2):
-            for k in range(8):
-                at = h * 64 + k * 8
-                piece = roll_lanes(load(RIM + half * 8 + k, h), at + (0 if side == 0 else RIM))
-                total = piece if total is None else jnp.where(group == h * 8 + k, piece, total)
-        return total
-
-    for half in range(2):
-        for side in range(2):
-            for c in range(3):
-                pack_own[side, half, c] = packed(lambda r, h: own[r, h, c], half, side)
-            pack_own[side, half, 3] = packed(
-                lambda r, h: reg[r, h].astype(jnp.float32), half, side
-            )
+    def add_to_pack(pack, c, load, first, count):
+        for half in range(2):
+            for side in range(2):
+                total = pack[side, half, c] if first else None
+                for h in range(2):
+                    for k in range(first, first + count):
+                        at = h * 64 + k * 8 + (0 if side == 0 else RIM)
+                        piece = roll_lanes(load(RIM + half * 8 + k, h), at)
+                        if total is None:
+                            total = piece
+                        else:
+                            total = jnp.where(group == h * 8 + k, piece, total)
+                pack[side, half, c] = total
 
     copies = []
 
@@ -190,7 +185,14 @@
             send(pack.at[0], rim.at[1, pl.ds(1, 2)], (img, left, gy)),
         ]
 
-    own_rims = send_packs(pack_own, rim_own) + send_rows(own, 0, RIM) + send_rows(reg, 0, RIM)
+    pltpu.make_async_copy(own.at[inner], own.at[inner], load_sem.at[0]).wait()
+    own_rims = send_rows(own, 0, RIM)
+    pltpu.make_async_copy(reg.at[inner], reg.at[inner], load_sem.at[1]).wait()
+    own_rims += send_rows(reg, 0, RIM)
+    for c in range(3):
+        add_to_pack(pack_own, c, lambda r, h: own[r, h, c], 0, 8)
+    add_to_pack(pack_own, 3, lambda r, h: reg[r, h].astype(jnp.float32), 0, 8)
+    own_rims += send_packs(pack_own, rim_own)
 
     heard(round_sem.at[0])
     tell(round_sem.at[1])
@@ -228,7 +230,7 @@
         copy.wait()
     low_image = lower[img]
     use_above = jnp.full((8, LANES), low_image, jnp.int32) == img
-    partner_rims = []
+    partner_rows = []
     for q in range(CHUNKS):
         for copy in late[q]:
             copy.wait_recv()
@@ -236,14 +238,12 @@
             for h in range(2):
                 for c in range(3):
                     partner[RIM + r, h, c] = jnp.where(use_above, above[r, h, c], below[r, h, c])
-        partner_rims += send_rows(partner, q * step, step)
-    for half in range(2):
-        for side in range(2):
-            for c in range(3):
-                pack_partner[side, half, c] = packed(
-                    lambda r, h: partner[r, h, c], half, side
-                )
-    partner_rims += send_packs(pack_partner, rim_partner)
+        if q < CHUNKS - 1:
+            partner_rows += send_rows(partner, q * step, step)
+        for c in range(3):
+            add_to_pack(pack_partner, c, lambda r, h: partner[r, h, c], q * step, step)
+    partner_packs = send_packs(pack_partner, rim_partner)
+    partner_rows += send_rows(partner, HALF - step, step)
 
     whole = pltpu.make_async_remote_copy(
         src_ref=red_buf, dst_ref=red_buf, send_sem=red_sem.at[0], recv_sem=red_sem.at[1],
@@ -258,18 +258,19 @@
             recv_sem=red_sem.at[3], device_id=line_peer(d), device_id_type=MESH,
         ).start()
 
-    def assembled(i, k, h, load, load_rim, upper):
-        at_a, at_b = h * 64 + k * 8, h * 64 + (7 - k) * 8
-        group_a, group_b = (0, 3) if upper else (1, 2)
+    def inner_part(i, h, load):
         a, b = load(i, h), load(EXT - 1 - i, h)
-        v = roll_lanes(load_rim(1, group_b), 120 - at_b)
-        v = jnp.where(lane < 120, roll_lanes(b, 120), v)
-        v = jnp.where(lane < 96, roll_lanes(b, 72), v)
-        v = jnp.where(lane < 72, roll_lanes(load_rim(0, group_b), 64 - at_b), v)
-        v = jnp.where(lane < 64, roll_lanes(load_rim(1, group_a), 56 - at_a), v)
-        v = jnp.where(lane < 56, roll_lanes(a, 56), v)
-        v = jnp.where(lane < 32, roll_lanes(a, 8), v)
-        return jnp.where(lane < 8, roll_lanes(load_rim(0, group_a), -at_a), v)
+        v = jnp.where(lane < 96, roll_lanes(b, 72), roll_lanes(b, 120))
+        v = jnp.where(lane < 64, roll_lanes(a, 56), v)
+        return jnp.where(lane < 32, roll_lanes(a, 8), v)
+
+    def with_rims(v, i, h, load_rim):
+        at_a, at_b = h * 64 + (i % 8) * 8, h * 64 + (7 - i % 8) * 8
+        group_a, group_b = (0, 3) if i < 8 else (1, 2)
+        v = jnp.where(group == 0, roll_lanes(load_rim(0, group_a), -at_a), v)
+        v = jnp.where(group == 7, roll_lanes(load_rim(1, group_a), 56 - at_a), v)
+        v = jnp.where(group == 8, roll_lanes(load_rim(0, group_b), 64 - at_b), v)
+        return jnp.where(group == 15, roll_lanes(load_rim(1, group_b), 120 - at_b), v)
 
     def put_coef(ref, i, h, region):
         aniso = jnp.zeros((8, LANES), jnp.float32)
@@ -293,34 +294,25 @@
     lax.fori_loop(0, EXT, main_coefs, 0)
     for i in range(ROWS):
         for h in range(2):
-            region = assembled(
-                i, i % 8, h,
-                lambda r, h: reg[r, h].astype(jnp.float32),
-                lambda side, g: rim_own[side, g, 3],
-                i < 8,
+            region = with_rims(
+                inner_part(i, h, lambda r, h: reg[r, h].astype(jnp.float32)),
+                i, h, lambda side, g: rim_own[side, g, 3],
             )
             put_coef(strip_coef, i, h, region.astype(jnp.int32))
 
-    def assemble(into, field, rim):
-        for i in range(ROWS):
-            for h in range(2):
-                for c in range(3):
-                    into[i, h, c] = assembled(
-                        i, i % 8, h, lambda r, h: field[r, h, c], lambda side, g: rim[side, g, c],
-                        i < 8,
-                    )
-
-    assemble(own_strip, own, rim_own)
+    for i in range(ROWS):
+        for h in range(2):
+            for c in range(3):
+                own_strip[i, h, c] = with_rims(
+                    inner_part(i, h, lambda r, h: own[r, h, c]),
+                    i, h, lambda side, g: rim_own[side, g, c],
+                )
 
     share = jnp.float32(0.0)
     share_all = jnp.float32(0.0)
     for n in range(n_img - 1):
         share = share + jnp.where(n < img, weights[n], 0.0)
         share_all = share_all + weights[n]
-
-    for copy in partner_rims:
-        copy.wait_recv()
-    assemble(partner_strip, partner, rim_partner)
 
     whole_line = pltpu.make_async_remote_copy(
         src_ref=line_buf, dst_ref=line_buf, send_sem=red_sem.at[2], recv_sem=red_sem.at[3],
@@ -341,20 +333,39 @@
     own_part = jnp.where(use_above, 1.0 - weight, weight)
     partner_part = jnp.where(use_above, weight, 1.0 - weight)
 
-    def start(into, ours, theirs, count):
-        def step(r, carry):
-            for h in range(2):
-                v = unit([
-                    own_part * ours[r, h, c] + partner_part * theirs[r, h, c] for c in range(3)
-                ])
-                for c in range(3):
-                    into[r, h, c] = v[c]
-            return carry
-
-        lax.fori_loop(0, count, step, 0, unroll=8)
-
-    start(strip, own_strip, partner_strip, ROWS)
-    start(main, own, partner, EXT)
+    def mixed(ours, theirs):
+        return unit([own_part * a + partner_part * b for a, b in zip(ours, theirs)])
+
+    for copy in partner_rows:
+        copy.wait_recv()
+
+    def start_row(r, carry):
+        for h in range(2):
+            v = mixed([own[r, h, c] for c in range(3)], [partner[r, h, c] for c in range(3)])
+            for c in range(3):
+                main[r, h, c] = v[c]
+        return carry
+
+    lax.fori_loop(0, EXT, start_row, 0, unroll=8)
+    for i in range(ROWS):
+        for h in range(2):
+            for c in range(3):
+                partner_strip[i, h, c] = inner_part(i, h, lambda r, h: partner[r, h, c])
+    for copy in partner_packs:
+        copy.wait_recv()
+    for i in range(ROWS):
+        for h in range(2):
+            v = mixed(
+                [own_strip[i, h, c] for c in range(3)],
+                [
+                    with_rims(
+                        partner_strip[i, h, c], i, h, lambda side, g: rim_partner[side, g, c]
+                    )
+                    for c in range(3)
+                ],
+            )
+            for c in range(3):
+                strip[i, h, c] = v[c]
     fold(strip)
 
     for copy in copies + early + sum(late, []):

time: 35.6 us -> 34.2 us (0.961)
  Pallas kernels: 35.4 us -> 34.1 us
    pallas_call x1, Pallas kernels: 29.5 us -> 28.2 us  [body(): pl.pallas_call(lambda *refs: exchange(shape, *refs), out_shape=[pltpu.VME...]
where the time goes in v7:
time: 34.2 us; the launch traced here: 34.1 us
  Pallas kernels  34.1 us (100%)
    pallas_call x1, Pallas kernels, body(): pl.pallas_call(lambda *refs: exchange(shape, *refs), out_shape=[pltpu.VME...  28.2 us
    pallas_call x1, Pallas kernels, body(): pl.pallas_call(evolve, out_shape=jax.ShapeDtypeStruct((3, 8, 2, ROWS, 1,...  5.92 us

profile of v7, /device:TPU:1, one launch (start us, length us, event | category | flops | bytes accessed | tf_op | source)
XLA Modules:
  0.0 34.1 jit_solution(16103131374403859406)
XLA Ops:
  0.0 28.2 %shard_map.64 = (f32[32,2,3,8,128]{4,3,2,1,0:T(8,128)S(1)}, f32[32,2,3,8,128]{4,3,2,1,0:T(8,128)S(1)}, f32[17,2,3,8,128]{4,3,2,1,0:T(8,128)S(1)}, f32[16,2,3,8,128]{4,3,2,1,0:T(8,128)S(1)}) custom-call(f32[3,8,2,16,1,128]{5,4,3,2,1,0:T(1,128)} %bitcast.3, s32[8,2,16,1,128]{4,3,2,1,0:T(1,128)} %bitcast.4, s32[16]{0:T(128)} %refs_2_.1, f32[15]{0:T(128)} %refs_3_.1, ...), custom_call_target="tpu_custom_call" | custom-call | tf_op jit(solution)/shard_map/pallas_call | solution.py:485
  28.2 5.9 %shard_map.65 = f32[3,8,2,16,1,128]{5,4,3,2,1,0:T(1,128)} custom-call(f32[32,2,3,8,128]{4,3,2,1,0:T(8,128)S(1)} %get-tuple-element.9.main_in, f32[32,2,3,8,128]{4,3,2,1,0:T(8,128)S(1)} %get-tuple-element.10.main_coef, f32[17,2,3,8,128]{4,3,2,1,0:T(8,128)S(1)} %get-tuple-element.11.strip_in, f32[16,2,3,8,128]{4,3,2,1,0:T(8,128)S(1)} %get-tuple-element.12.strip_coef), custom_call_target="tpu_custom_call" | custom-call | tf_op jit(solution)/shard_map/pallas_call | solution.py:527

commit v8 on v7

--- a/solution.py
+++ b/solution.py
@@ -54,11 +54,11 @@
     prev, nxt = lax.rem(img + n_img - 1, n_img), lax.rem(img + 1, n_img)
 
     plane = Y_LO * n_gx * n_gy
-    me_plane = (y_lo * n_gx + gx) * n_gy + gy
 
     def plane_peer(d):
-        t = lax.rem(me_plane + d, plane)
-        return ((t // (n_gx * n_gy)) * n_z + z, (t // n_gy) % n_gx, t % n_gy)
+        a, b, c = d // (n_gx * n_gy), (d // n_gy) % n_gx, d % n_gy
+        there = lax.rem(y_lo + a, Y_LO) * n_z + z
+        return (there, lax.rem(gx + b, n_gx), lax.rem(gy + c, n_gy))
 
     def line_peer(d):
         return (y_lo * n_z + lax.rem(z + d, n_z), gx, gy)
@@ -211,20 +211,21 @@
         return first, second
 
     zero = jnp.zeros((8, LANES), jnp.float32)
-    first, second = lax.fori_loop(0, HALF, add_squares, (zero, zero))
+    first, second = lax.fori_loop(0, HALF, add_squares, (zero, zero), unroll=4)
     heard(round_sem.at[1])
-    tell(round_sem.at[2])
     row_lane = lax.broadcasted_iota(jnp.int32, (1, LANES), 1)
     first, second = (
         jnp.sum(jnp.sum(v, axis=0, keepdims=True), axis=1, keepdims=True) for v in (first, second)
     )
     partial = jnp.where(row_lane == img, first, 0.0)
     red_src[...] = partial + jnp.where(row_lane == img + 1, second, 0.0)
-    for d in range(1, plane):
+    for d in sorted(range(1, plane), key=lambda d: -min(d % n_gy, n_gy - d % n_gy)):
         pltpu.make_async_remote_copy(
             src_ref=red_src, dst_ref=red_buf.at[d - 1], send_sem=red_sem.at[0],
             recv_sem=red_sem.at[1], device_id=plane_peer(d), device_id_type=MESH,
         ).start()
+
+    tell(round_sem.at[2])
 
     for copy in tables:
         copy.wait()
@@ -252,7 +253,7 @@
     whole.wait_recv()
     heard(round_sem.at[2])
     line_src[...] = red_src[...] + jnp.sum(red_buf[...], axis=0)
-    for d in range(1, n_z):
+    for d in sorted(range(1, n_z), key=lambda d: -min(d, n_z - d)):
         pltpu.make_async_remote_copy(
             src_ref=line_src, dst_ref=line_buf.at[d - 1], send_sem=red_sem.at[2],
             recv_sem=red_sem.at[3], device_id=line_peer(d), device_id_type=MESH,

time: 34.2 us -> 34.3 us (level)
  no operation moved by 1% of the time
where the time goes in v8:
time: 34.3 us; the launch traced here: 34.1 us
  Pallas kernels  34.1 us (99%)
    pallas_call x1, Pallas kernels, body(): pl.pallas_call(lambda *refs: exchange(shape, *refs), out_shape=[pltpu.VME...  28.2 us
    pallas_call x1, Pallas kernels, body(): pl.pallas_call(evolve, out_shape=jax.ShapeDtypeStruct((3, 8, 2, ROWS, 1,...  5.92 us

profile of v8, /device:TPU:1, one launch (start us, length us, event | category | flops | bytes accessed | tf_op | source)
XLA Modules:
  0.0 34.1 jit_solution(7928108209920333622)
XLA Ops:
  0.0 28.2 %shard_map.64 = (f32[32,2,3,8,128]{4,3,2,1,0:T(8,128)S(1)}, f32[32,2,3,8,128]{4,3,2,1,0:T(8,128)S(1)}, f32[17,2,3,8,128]{4,3,2,1,0:T(8,128)S(1)}, f32[16,2,3,8,128]{4,3,2,1,0:T(8,128)S(1)}) custom-call(f32[3,8,2,16,1,128]{5,4,3,2,1,0:T(1,128)} %bitcast.3, s32[8,2,16,1,128]{4,3,2,1,0:T(1,128)} %bitcast.4, s32[16]{0:T(128)} %refs_2_.1, f32[15]{0:T(128)} %refs_3_.1, ...), custom_call_target="tpu_custom_call" | custom-call | tf_op jit(solution)/shard_map/pallas_call | solution.py:486
  28.2 5.9 %shard_map.65 = f32[3,8,2,16,1,128]{5,4,3,2,1,0:T(1,128)} custom-call(f32[32,2,3,8,128]{4,3,2,1,0:T(8,128)S(1)} %get-tuple-element.9.main_in, f32[32,2,3,8,128]{4,3,2,1,0:T(8,128)S(1)} %get-tuple-element.10.main_coef, f32[17,2,3,8,128]{4,3,2,1,0:T(8,128)S(1)} %get-tuple-element.11.strip_in, f32[16,2,3,8,128]{4,3,2,1,0:T(8,128)S(1)} %get-tuple-element.12.strip_coef), custom_call_target="tpu_custom_call" | custom-call | tf_op jit(solution)/shard_map/pallas_call | solution.py:528
